TPU v7x, 32 devices: a whole 2x2x4 slice. The times are simulated.
32 devices in a mesh: lon: 16 (over z, x, core), lev: 2 (over y).
Axes of the slice: x: 2, y: 2, z: 4, core: 2. Of those that a mesh axis runs over, the one named last changes fastest.
Arguments:
- cotangent: float32 [5, 8, 2880, 1024], P(None, 'lev', 'lon'), may hold values from -6 to 6
- zonal_coef: float32 [8, 2880, 1024], P('lev', 'lon'), may hold values from -0.5 to 0.5
- merid_coef: float32 [8, 2880, 1024], P('lev', 'lon'), may hold values from -0.5 to 0.5
- vertical_wind: float32 [8, 2880, 1024], P('lev', 'lon'), may hold values from -0.5 to 0.5
- cutoff: int32 [64], replicated, may hold values from 1 to 360, as said below
Outputs:
- adjoint_state: float32 [5, 8, 2880, 1024], P(None, 'lev', 'lon')
Inputs may be any that keep to these rules, and one draw needn't show every extreme that they name: Every draw holds a row with cutoff exactly 360 and a row with cutoff exactly 1.
All inputs are finite; a program needn't handle non-finite values.
Results may differ from a plain program's by a relative error of at most 0.00023.
Values sent between devices are 32-bit elements; how exact they have to be, the bound alone decides.
A program may use at most 192 MiB of HBM per device.

v0:
```python
import math

import jax
import jax.numpy as jnp
from jax import lax
from jax.sharding import PartitionSpec as P

NLON = 2880
POLAR = 32


COUPLE_G = 0.3
COUPLE_H = 0.3
COUPLE_B = 0.2


def with_halo(shard, sides, width):
    for axis, dim in sides:
        peers, length = (lax.axis_size(axis), shard.shape[dim])
        up = [(i, (i + 1) % peers) for i in range(peers)]
        down = [(j, i) for i, j in up]
        last = lax.slice_in_dim(shard, length - width, length, axis=dim)
        initial = lax.slice_in_dim(shard, 0, width, axis=dim)
        before = lax.ppermute(last, axis, up)
        after = lax.ppermute(initial, axis, down)
        shard = jnp.concatenate([before, shard, after], axis=dim)
    return shard


def reverse_cumsum(values):
    return jnp.flip(jnp.cumsum(jnp.flip(values, 0), 0), 0)


def column_update(adjoint, level_diff, below_sums):
    updated = adjoint + level_diff
    return updated.at[3].add(-COUPLE_B * below_sums)


def dirichlet(offsets, cut_rows):
    odd_count = 2 * cut_rows + 1
    phase = odd_count[None, None, :] * offsets[:, :, None] % (2 * NLON)
    numerator = jnp.sin(math.pi * phase.astype(jnp.float32) / NLON)
    sine_base = jnp.sin(math.pi * offsets.astype(jnp.float32) / NLON)
    safe_base = jnp.where(offsets == 0, 1.0, sine_base)
    general = numerator / (NLON * safe_base[:, :, None])
    centre = odd_count.astype(jnp.float32)[None, None, :] / NLON
    return jnp.where((offsets == 0)[:, :, None], centre, general)


def body(cotangent, zonal_coef, merid_coef, vertical_wind, cutoff):
    lon_dev = cotangent.shape[2]
    lat_rows = cotangent.shape[3]
    packed = jnp.concatenate([cotangent, vertical_wind[None]], 0)
    columns = lax.all_to_all(packed, "lev", split_axis=3, concat_axis=1, tiled=True)
    column_adj = columns[:5]
    weighted = columns[5][None] * column_adj
    padded = jnp.pad(weighted, ((0, 0), (1, 1), (0, 0), (0, 0)))
    updated = column_update(
        column_adj, padded[:, 2:] - padded[:, :-2], reverse_cumsum(column_adj[2])
    )
    adjoint_one = lax.all_to_all(updated, "lev", split_axis=1, concat_axis=3, tiled=True)
    polar_rows = jnp.concatenate(
        [adjoint_one[..., :POLAR], adjoint_one[..., lat_rows - POLAR :]], axis=3
    )
    mine = lax.axis_index("lon") * lon_dev + jnp.arange(lon_dev, dtype=jnp.int32)
    piece = lax.all_gather(polar_rows, "lon", axis=2, tiled=True)
    theirs = jnp.arange(piece.shape[2], dtype=jnp.int32)
    offsets = (mine[:, None] - theirs[None, :]) % NLON
    kernel = dirichlet(offsets, cutoff)
    smoothed = jnp.einsum("fapj,lpj->falj", piece, kernel, precision=lax.Precision.HIGHEST)
    filtered = jnp.concatenate(
        [smoothed[..., :POLAR], adjoint_one[..., POLAR : lat_rows - POLAR], smoothed[..., POLAR:]],
        axis=3,
    )
    zonal_part = zonal_coef[None] * filtered
    zonal_flux = jnp.stack(
        [
            zonal_part[0] + COUPLE_H * filtered[3],
            zonal_part[1],
            zonal_part[2],
            zonal_part[3] + COUPLE_G * filtered[0],
            zonal_part[4],
        ]
    )
    merid_part = merid_coef[None] * filtered
    merid_flux = jnp.stack(
        [
            merid_part[0],
            merid_part[1] + COUPLE_H * filtered[3],
            merid_part[2],
            merid_part[3] + COUPLE_G * filtered[1],
            merid_part[4],
        ]
    )
    zonal_padded = with_halo(zonal_flux, (("lon", 2),), 1)
    zonal_diff = zonal_padded[:, :, 2:] - zonal_padded[:, :, :-2]
    merid_padded = jnp.pad(merid_flux, ((0, 0), (0, 0), (0, 0), (1, 1)))
    merid_diff = merid_padded[..., 2:] - merid_padded[..., :-2]
    return adjoint_one + zonal_diff + merid_diff


def solution(mesh):
    return jax.shard_map(
        body,
        mesh=mesh,
        in_specs=(
            P(None, "lev", "lon", None),
            P("lev", "lon", None),
            P("lev", "lon", None),
            P("lev", "lon", None),
            P(),
        ),
        out_specs=P(None, "lev", "lon", None),
        check_vma=False,
    )
```

profile of v0, /device:TPU:27, one launch (start us, length us, event | category | flops | bytes accessed | tf_op | source)
XLA Modules:
  0.0 1754.2 jit_solution(14034547264191298171)
XLA Ops:
  6.5 28.8 %copy.59 = f32[5,4,180,1024]{2,1,0,3:T(4,128)} copy(f32[5,4,180,1024]{3,1,2,0:T(4,128)} %param.7) | data formatting | bytes 29491200 | tf_op args[0]
  35.3 7.0 copy.58
  42.3 14.2 pad_maximum_fusion
  56.6 278.4 %all_to_all.33 = f32[6,4,180,1024]{2,1,0,3:T(4,128)} all-to-all(f32[6,4,180,1024]{2,1,0,3:T(4,128)S(1)} %pad_maximum_fusion), channel_id=1, replica_groups=mesh['lon'=16,'lev'=2] {'lev'}, dimensions={3} | all-to-all | bytes 35389440 | tf_op jit(solution)/shard_map/all_to_all | solution.py:54
  335.0 26.2 %copy.60 = f32[6,4,180,2,512]{4,2,1,3,0:T(8,128)} copy(f32[6,4,180,2,512]{2,1,0,4,3:T(4,128)} %bitcast.34) | data formatting | bytes 35389440 | tf_op jit(solution)/shard_map/all_to_all | solution.py:54
  361.2 13.0 slice.152
  377.8 12.6 broadcast_multiply_fusion
  390.4 14.4 fusion.23
  413.0 12.8 copy.61
  425.8 168.3 %all_to_all.34 = f32[5,8,180,512]{3,2,0,1:T(8,128)S(1)} all-to-all(f32[5,8,180,512]{3,2,0,1:T(8,128)} %copy.61), channel_id=1, replica_groups=mesh['lon'=16,'lev'=2] {'lev'}, dimensions={1} | all-to-all | bytes 29491200 | tf_op jit(solution)/shard_map/all_to_all | solution.py:61
  594.1 16.5 copy.63
  610.6 18.3 %all_to_all.30 = f32[5,4,180,1024]{3,2,1,0:T(8,128)} reshape(f32[5,4,180,2,512]{4,3,2,1,0:T(2,128)} %copy.63) | data formatting | bytes 29491200 | tf_op jit(solution)/shard_map/all_to_all | solution.py:61
  637.7 10.0 select_multiply_fusion
  647.7 14.9 slice.159
  662.6 12.7 copy.67
  675.3 108.8 %all-gather.2.cloned.1.call-done = f32[5,4,2880,64]{3,1,0,2:T(4,128)} async-done(((f32[5,4,180,64]{3,1,0,2:T(4,128)}), f32[5,4,2880,64]{3,1,0,2:T(4,128)}) %all-gather.2.cloned.1.call-update) | async-done | bytes 14745616 | tf_op jit(solution)/shard_map/all_gather | solution.py:66
  784.2 31.2 %copy.65 = f32[5,4,2880,64]{2,0,1,3:T(8,128)} copy(f32[5,4,2880,64]{3,1,0,2:T(4,128)} %all-gather.2.cloned.1.call-done) | data formatting | bytes 29491200 | tf_op jit(solution)/shard_map/all_gather | solution.py:66
  815.4 777.2 %fusion.33 = f32[5,4,180,64]{2,0,1,3:T(8,128)S(1)} fusion(f32[5,4,2880,64]{2,0,1,3:T(8,128)} %copy.65, f32[180,2880]{1,0:T(8,128)} %select_multiply_fusion, s32[180,2880]{1,0:T(8,128)S(1)} %add_select_fusion.1, s32[64]{0:T(128)S(1)} %multiply_add_fusion, f32[64]{0:T(128)S(1)} %convert_multiply_fusion, pred[180,2880]{1,0:T(8,128)(4,1)S(1)} %broadcast_compare_fusion), kind=kOutput, calls=%fused_computation.64 | convolution fusion | flops 8327577600 | bytes 20333312 | tf_op jit(solution)/shard_map/fapj,lpj->falj/dot_general | solution.py:70
  1597.9 18.2 %broadcast_multiply_fusion.2 = (f32[5,4,180,1024]{3,1,2,0:T(4,128)}, f32[5,4,180,1024]{3,1,2,0:T(4,128)S(1)}) fusion(f32[4,180,1024]{2,0,1:T(4,128)} %param.8, f32[5,4,180,32]{3,1,2,0:T(4,128)} %copy.68, f32[5,4,180,960]{3,1,2,0:T(4,128)} %copy.67, f32[5,4,180,32]{3,1,2,0:T(4,128)S(1)} %copy.66), kind=kLoop, calls=%fused_computation.42 | loop fusion | flops 11059200 | bytes 47185920 | tf_op jit(solution)/shard_map/mul | solution.py:75
  1640.3 11.9 slice_add_fusion.2
  1661.8 19.0 %copy.71 = f32[5,4,180,1024]{3,2,1,0:T(8,128)} copy(f32[5,4,180,1024]{3,1,2,0:T(4,128)} %slice_dynamic-update-slice_fusion) | data formatting | bytes 29491200 | tf_op jit(solution)/shard_map/stack | solution.py:86
  1680.8 23.4 %pad_maximum_fusion.5 = (f32[5,4,180,1024]{3,1,2,0:T(4,128)}, f32[5,4,180,1024]{3,1,2,0:T(4,128)}) fusion(f32[5,4,1,1024]{3,1,2,0:T(4,128)S(1)} %collective-permute-done, f32[1,4,180,1024]{3,1,2,0:T(4,128)} %get-tuple-element.30, f32[1,4,180,1024]{3,1,2,0:T(4,128)} %get-tuple-element.20, f32[2,4,180,1024]{3,1,2,0:T(4,128)} %copy-done.2, ...), kind=kLoop, calls=%fused_computation.35 | loop fusion | flops 29491200 | bytes 44400640 | tf_op jit(solution)/shard_map/concatenate | solution.py:26
  1704.2 30.4 %fusion.21 = f32[5,4,180,1024]{3,2,1,0:T(8,128)} fusion(f32[5,4,180,1024]{3,2,1,0:T(8,128)S(1)} %copy-done, f32[5,4,180,1024]{3,2,1,0:T(8,128)} %all_to_all.30, f32[5,4,180,1024]{3,1,2,0:T(4,128)} %get-tuple-element.26, f32[5,4,180,1024]{3,1,2,0:T(4,128)} %get-tuple-element.25), kind=kLoop, calls=%fused_computation.26 | loop fusion | flops 14745600 | bytes 73728000 | tf_op jit(solution)/shard_map/add | solution.py:99
  1734.6 12.6 copy.72
  (49 shorter events, 59.5 us)
Async XLA Ops:
  6.5 28.8 %copy-start.4 = (f32[4,180,1024]{2,0,1:T(4,128)S(1)}, f32[4,180,1024]{2,0,1:T(4,128)}, u32[]{:S(2)}) copy-start(f32[4,180,1024]{2,0,1:T(4,128)} %param.10) | copy-start | bytes 8847364
  6.5 777.6 %all-gather.2.cloned.1.call-start = ((), (), s32[]{:S(2)}) async-start(), calls=%async_computation.2 | async-start | bytes 31334400 | tf_op jit(solution)/shard_map/all_gather | solution.py:66
  374.1 16.3 slice-start
  374.2 16.3 slice-start.1
  377.8 12.6 slice-start.2
  377.8 12.6 slice-start.3
  628.8 5.1 copy-start.5
  1619.8 5.1 copy-start.1
  1640.3 11.9 copy-start.2
  1653.1 27.7 %collective-permute-start = (f32[5,4,1,1024]{3,1,2,0:T(4,128)S(1)}, f32[5,4,1,1024]{3,1,2,0:T(4,128)S(1)}, u32[]{:S(2)}, u32[]{:S(2)}) collective-permute-start(f32[5,4,1,1024]{3,1,2,0:T(4,128)S(1)} %get-tuple-element.27), channel_id=1, source_target_pairs={{2,0},{4,2},{6,4},{8,6},{10,8},{12,10},{14,12},{16,14},{18,16},{20... | collective-permute-start | bytes 245768 | tf_op jit(solution)/shard_map/ppermute | solution.py:25
  1653.4 27.4 %collective-permute-start.1 = (f32[5,4,1,1024]{3,1,2,0:T(4,128)S(1)}, f32[5,4,1,1024]{3,1,2,0:T(4,128)S(1)}, u32[]{:S(2)}, u32[]{:S(2)}) collective-permute-start(f32[5,4,1,1024]{3,1,2,0:T(4,128)S(1)} %get-tuple-element.28), channel_id=1, source_target_pairs={{0,2},{2,4},{4,6},{6,8},{8,10},{10,12},{12,14},{14,16},{16,18},{18... | collective-permute-start | bytes 245768 | tf_op jit(solution)/shard_map/ppermute | solution.py:24
  1661.8 19.0 %copy-start.3 = (f32[1,4,180,1024]{3,1,2,0:T(4,128)S(1)}, f32[1,4,180,1024]{3,1,2,0:T(4,128)}, u32[]{:S(2)}) copy-start(f32[1,4,180,1024]{3,1,2,0:T(4,128)} %get-tuple-element.19) | copy-start | bytes 8847364
  1680.8 23.4 %copy-start = (f32[5,4,180,1024]{3,2,1,0:T(8,128)S(1)}, f32[5,4,180,1024]{3,2,1,0:T(8,128)}, u32[]{:S(2)}) copy-start(f32[5,4,180,1024]{3,2,1,0:T(8,128)} %copy.71) | copy-start | bytes 44236804
Sparse Core Ops, SparseCore 0:
  634.0 150.0 all-gather.1
where the time goes:
time: 1770 us; the launch traced here: 1750 us
  matrix products  777 us (44%)
  blocking collectives  447 us (25%)
  local copies, waits for them, and re-layouts  248 us (14%)
  other arithmetic  155 us (9%)
  waiting for transfers between devices  109 us (6%)
    dot_general x1, matrix products, body(): jnp.einsum('fapj,lpj->falj', piece, kernel, precision=lax.Precision.HIGHEST)  777 us
    all_to_all x1, blocking collectives, body(): lax.all_to_all(packed, 'lev', split_axis=3, concat_axis=1, tiled=True)  278 us
    all_to_all x1, blocking collectives, body(): lax.all_to_all(updated, 'lev', split_axis=1, concat_axis=3, tiled=True)  168 us
    all_gather x1, waiting for transfers between devices, body(): piece = lax.all_gather(polar_rows, 'lon', axis=2, tiled=True)  109 us
    unnamed x24, local copies, waits for them, and re-layouts  47.3 us
  transfers between devices with their start and end apart: 3, of which 1 were waited for; matrix products, arithmetic and copies ran while one was open for 4% of the time, Pallas kernels for 0%

commit v1 on v0

v1 whole, which is shorter than its diff:
```python
import functools
import math

import jax
import jax.numpy as jnp
from jax import lax
from jax.experimental import pallas as pl
from jax.experimental.pallas import tpu as pltpu
from jax.sharding import PartitionSpec as P

POLAR = 32
KMAX = 360
COUPLE_G = 0.3
COUPLE_H = 0.3
COUPLE_B = 0.2
WIDE = 256
MESH = pl.DeviceIdType.MESH
HIGHEST = lax.Precision.HIGHEST


def angles(left, right, period):
    turn = (left * right) % period
    phase = turn.astype(jnp.float32) * (2.0 * math.pi / period)
    return jnp.cos(phase), jnp.sin(phase)


def filter_kernel(
    peers, x_ref, fwd_ref, inv_ref, ct_ref, st_ref, mask_ref, out_ref, held, made,
    own_sem, send_a, recv_a, send_b, recv_b,
):
    me = lax.axis_index("lon")
    kpad = ct_ref.shape[2]
    barrier = pltpu.get_barrier_semaphore()

    def greet(o, _):
        pl.semaphore_signal(
            barrier, inc=1, device_id={"lon": lax.rem(me + o, peers)}, device_id_type=MESH
        )
        return 0

    lax.fori_loop(1, peers, greet, 0)
    pl.semaphore_wait(barrier, peers - 1)

    def out_copy(o):
        d = lax.rem(me + o, peers)
        return pltpu.make_async_remote_copy(
            src_ref=x_ref.at[d], dst_ref=held.at[me], send_sem=send_a.at[d],
            recv_sem=recv_a.at[me], device_id={"lon": d}, device_id_type=MESH,
        )

    def in_copy(o):
        s = lax.rem(me + o, peers)
        return pltpu.make_async_remote_copy(
            src_ref=x_ref.at[s], dst_ref=held.at[s], send_sem=send_a.at[s],
            recv_sem=recv_a.at[s], device_id={"lon": s}, device_id_type=MESH,
        )

    def back_copy(o):
        d = lax.rem(me + o, peers)
        return pltpu.make_async_remote_copy(
            src_ref=made.at[d], dst_ref=out_ref.at[me], send_sem=send_b.at[d],
            recv_sem=recv_b.at[me], device_id={"lon": d}, device_id_type=MESH,
        )

    def home_copy(o):
        s = lax.rem(me + o, peers)
        return pltpu.make_async_remote_copy(
            src_ref=made.at[s], dst_ref=out_ref.at[s], send_sem=send_b.at[s],
            recv_sem=recv_b.at[s], device_id={"lon": s}, device_id_type=MESH,
        )

    lax.fori_loop(1, peers, lambda o, c: (out_copy(o).start(), c)[1], 0)
    own = pltpu.make_async_copy(x_ref.at[me], held.at[me], own_sem)
    own.start()
    own.wait()
    lax.fori_loop(1, peers, lambda o, c: (in_copy(o).wait_recv(), c)[1], 0)

    cols = held.shape[1]
    zero = jnp.zeros((cols, kpad), jnp.float32)

    def gather(s, carry):
        a, b = carry
        both = jnp.dot(held[s], fwd_ref[...], precision=HIGHEST, preferred_element_type=jnp.float32)
        c, v = both[:, :kpad], both[:, kpad:]
        ct, st = ct_ref[s], st_ref[s]
        return a + (ct * c - st * v), b + (st * c + ct * v)

    a, b = lax.fori_loop(0, peers, gather, (zero, zero))
    a = a * mask_ref[...]
    b = b * mask_ref[...]

    def spread(d, carry):
        a, b = carry
        ct, st = ct_ref[d], st_ref[d]
        made[d] = jnp.dot(
            a * ct + b * st, inv_ref[0], precision=HIGHEST, preferred_element_type=jnp.float32
        ) + jnp.dot(
            b * ct - a * st, inv_ref[1], precision=HIGHEST, preferred_element_type=jnp.float32
        )
        return carry

    lax.fori_loop(0, peers, spread, (a, b))
    lax.fori_loop(1, peers, lambda o, c: (back_copy(o).start(), c)[1], 0)
    mine = pltpu.make_async_copy(made.at[me], out_ref.at[me], own_sem)
    mine.start()
    mine.wait()
    lax.fori_loop(1, peers, lambda o, c: (home_copy(o).wait_recv(), c)[1], 0)
    lax.fori_loop(1, peers, lambda o, c: (out_copy(o).wait_send(), c)[1], 0)
    lax.fori_loop(1, peers, lambda o, c: (back_copy(o).wait_send(), c)[1], 0)


def polar_filter(x, cutoff, peers):
    _, cols, lon_dev = x.shape
    nlon = peers * lon_dev
    rows = cutoff.shape[0] // peers
    kpad = (KMAX + 1 + 127) // 128 * 128
    wave = jnp.arange(kpad, dtype=jnp.int32)
    place = jnp.arange(lon_dev, dtype=jnp.int32)
    fwd = jnp.concatenate(angles(place[:, None], wave[None, :], nlon), axis=1)
    wide = jnp.arange(-1, lon_dev + 1, dtype=jnp.int32)
    inv = jnp.stack(angles(wave[:, None], wide[None, :] % nlon, nlon))
    seat = jnp.arange(peers, dtype=jnp.int32) * lon_dev
    ct, st = angles(seat[:, None, None], wave[None, None, :], nlon)
    mine = lax.dynamic_slice_in_dim(cutoff, lax.axis_index("lon") * rows, rows)
    weight = jnp.where(wave == 0, 1.0 / nlon, 2.0 / nlon)
    mask = jnp.where(wave[None, :] <= mine[:, None], weight[None, :], 0.0)
    mask = jnp.tile(mask, (cols // rows, 1))
    vmem = pl.BlockSpec(memory_space=pltpu.VMEM)
    dma = pltpu.SemaphoreType.DMA
    return pl.pallas_call(
        functools.partial(filter_kernel, peers),
        out_shape=jax.ShapeDtypeStruct((peers, cols, lon_dev + 2), jnp.float32),
        in_specs=[vmem] * 6,
        out_specs=vmem,
        scratch_shapes=[
            pltpu.VMEM((peers, cols, lon_dev), jnp.float32),
            pltpu.VMEM((peers, cols, lon_dev + 2), jnp.float32),
            dma(()), dma((peers,)), dma((peers,)), dma((peers,)), dma((peers,)),
        ],
        compiler_params=pltpu.CompilerParams(
            collective_id=0, has_side_effects=True, vmem_limit_bytes=24 << 20
        ),
        cost_estimate=pl.CostEstimate(flops=8_000_000_000, bytes_accessed=60_000_000, transcendentals=0),
        name="polar_filter",
    )(x, fwd, inv, ct, st, mask)


def coupled(coef, fields, first):
    flux = [coef * f for f in fields]
    flux[first] = flux[first] + COUPLE_H * fields[3]
    flux[3] = flux[3] + COUPLE_G * fields[first]
    return flux


def stencil_kernel(tiles, levels, n_edge, n_old, ids, flags, cot, vw, zc, mc, tail, smooth, halo, *rest):
    edges = rest[:n_edge]
    out, filt, done, rim = rest[n_edge + n_old :]
    t, i = pl.program_id(0), pl.program_id(1)
    k = ids[i]
    width = filt.shape[2]
    lon = filt.shape[1]

    @pl.when(t < tiles)
    def _():
        upper = jnp.minimum(k + 1, levels - 1)
        lower = jnp.maximum(k - 1, 0)
        wind_up = vw[upper] * flags[0, i]
        wind_dn = vw[lower] * flags[1, i]
        base = []
        for f in range(5):
            a = cot[f, k] + (wind_up * cot[f, upper] - wind_dn * cot[f, lower])
            for n, e in enumerate(edges):
                a = a + flags[2 + n, i] * e[f]
            if f == 3:
                below = tail[...]
                for m in range(levels):
                    below = below + jnp.where(m >= k, 1.0, 0.0) * cot[2, m]
                a = a - COUPLE_B * below
            base.append(a)
            filt[f] = a
        lane = lax.broadcasted_iota(jnp.int32, (lon, 128), 1)

        @pl.when(t == 0)
        def _():
            for f in range(5):
                filt[f, :, :128] = jnp.where(lane < POLAR, smooth[f, 0], filt[f, :, :128])

        @pl.when(t == tiles - 1)
        def _():
            for f in range(5):
                filt[f, :, width - 128 :] = jnp.where(
                    lane >= 128 - POLAR, smooth[f, 0], filt[f, :, width - 128 :]
                )

        fields = [filt[f] for f in range(5)]
        zonal = coupled(zc[0], fields, 0)
        merid = coupled(mc[0], fields, 1)
        place = lax.broadcasted_iota(jnp.int32, (lon, width), 1)
        for f in range(5):
            ahead = jnp.concatenate([zonal[f][1:], halo[f, 0, 1:2]], 0)
            behind = jnp.concatenate([halo[f, 0, 0:1], zonal[f][:-1]], 0)
            total = base[f] + (ahead - behind)
            right = jnp.concatenate([merid[f][:, 1:], merid[f][:, :1]], 1)
            left = jnp.concatenate([merid[f][:, width - 1 :], merid[f][:, : width - 1]], 1)
            out[f, 0] = done[i, f] + jnp.where(place == width - 1, right, 0.0)
            total = total + jnp.where(place == width - 1, 0.0, right)
            edge = jnp.where(t > 0, rim[i, f], 0.0)
            rim[i, f] = left[:, :128]
            head = jnp.where(lane == 0, edge, left[:, :128])
            left = jnp.concatenate([head, left[:, 128:]], 1) if width > 128 else head
            done[i, f] = total - left

    @pl.when(t == tiles)
    def _():
        out[:, 0] = done[i]


def stencil(ids, flags, cot, vw, zc, mc, tail, smooth, halo, edges, old):
    _, levels, lon, lat = cot.shape
    width = WIDE
    tiles = lat // width
    nk = ids.shape[0]
    last = lambda t: jnp.minimum(t, tiles - 1)
    level = lambda t, i, ids: jnp.where(t == tiles, ids[nk - 1], ids[i])
    in_specs = [
        pl.BlockSpec((5, levels, lon, width), lambda t, i, ids, fl: (0, 0, 0, last(t))),
        pl.BlockSpec((levels, lon, width), lambda t, i, ids, fl: (0, 0, last(t))),
        pl.BlockSpec((1, lon, width), lambda t, i, ids, fl: (level(t, i, ids), 0, last(t))),
        pl.BlockSpec((1, lon, width), lambda t, i, ids, fl: (level(t, i, ids), 0, last(t))),
        pl.BlockSpec((lon, width), lambda t, i, ids, fl: (0, last(t))),
        pl.BlockSpec((5, 1, lon, 128), lambda t, i, ids, fl: (0, level(t, i, ids), 0, jnp.where(t < tiles - 1, 0, 1))),
        pl.BlockSpec((5, 1, 2, width), lambda t, i, ids, fl: (0, level(t, i, ids), 0, last(t))),
    ]
    in_specs += [pl.BlockSpec((5, lon, width), lambda t, i, ids, fl: (0, 0, last(t)))] * len(edges)
    args = [cot, vw, zc, mc, tail, smooth, halo, *edges]
    aliases = {}
    if old is not None:
        in_specs.append(pl.BlockSpec(memory_space=pl.ANY))
        args.append(old)
        aliases = {2 + len(args) - 1: 0}
    return pl.pallas_call(
        functools.partial(stencil_kernel, tiles, levels, len(edges), int(old is not None)),
        out_shape=jax.ShapeDtypeStruct(cot.shape, jnp.float32),
        grid_spec=pltpu.PrefetchScalarGridSpec(
            num_scalar_prefetch=2,
            grid=(tiles + 1, nk),
            in_specs=in_specs,
            out_specs=pl.BlockSpec(
                (5, 1, lon, width),
                lambda t, i, ids, fl: (0, jnp.where(t == 0, ids[0], ids[i]), 0, jnp.maximum(t - 1, 0)),
            ),
            scratch_shapes=[
                pltpu.VMEM((5, lon, width), jnp.float32),
                pltpu.VMEM((nk, 5, lon, width), jnp.float32),
                pltpu.VMEM((nk, 5, lon, 128), jnp.float32),
            ],
        ),
        input_output_aliases=aliases,
        compiler_params=pltpu.CompilerParams(vmem_limit_bytes=56 << 20),
        cost_estimate=pl.CostEstimate(
            flops=30 * nk * 5 * lon * lat, bytes_accessed=4 * nk * 13 * lon * lat, transcendentals=0
        ),
        name="stencil",
    )(ids, flags, *args)


def swap_levels(first, last):
    count = lax.axis_size("lev")
    if count == 2:
        seat = lax.axis_index("lev")
        got = lax.ppermute(jnp.where(seat == 0, last, first), "lev", [(0, 1), (1, 0)])
        return jnp.where(seat == 0, got, 0.0), jnp.where(seat == 1, got, 0.0)
    up = lax.ppermute(first, "lev", [(i + 1, i) for i in range(count - 1)])
    down = lax.ppermute(last, "lev", [(i, i + 1) for i in range(count - 1)])
    return up, down


def later_sum(local):
    count = lax.axis_size("lev")
    total = jnp.zeros_like(local)
    for r in range(1, count):
        total = total + lax.ppermute(local, "lev", [(i + r, i) for i in range(count - r)])
    return total


def adjoint_part(cot, vw):
    weighted = vw[None] * cot
    up, down = swap_levels(weighted[:, 0], weighted[:, -1])
    above = jnp.concatenate([weighted[:, 1:], up[:, None]], 1)
    under = jnp.concatenate([down[:, None], weighted[:, :-1]], 1)
    below = jnp.flip(jnp.cumsum(jnp.flip(cot[2], 0), 0), 0) + later_sum(cot[2].sum(0))[None]
    return (cot + (above - under)).at[3].add(-COUPLE_B * below)


def polar_cut(x):
    return jnp.concatenate([x[..., :POLAR], x[..., x.shape[-1] - POLAR :]], -1)


def body(cotangent, zonal_coef, merid_coef, vertical_wind, cutoff):
    levels, lon_dev, lat = cotangent.shape[1:]
    peers = lax.axis_size("lon")
    count = lax.axis_size("lev")
    seat = lax.axis_index("lev")

    polar_cot = jnp.swapaxes(polar_cut(cotangent), 2, 3)
    polar_vw = jnp.swapaxes(polar_cut(vertical_wind), 1, 2)
    polar = adjoint_part(polar_cot, polar_vw)
    rows = 2 * POLAR // peers
    grouped = polar.reshape(5 * levels, peers, rows, lon_dev)
    grouped = jnp.swapaxes(grouped, 0, 1).reshape(peers, 5 * levels * rows, lon_dev)

    ends = []
    for at in (lon_dev - 1, 0):
        ends.append(
            jnp.concatenate(
                [cotangent[:, :, at].reshape(5 * levels, lat), vertical_wind[:, at], zonal_coef[:, at]], 0
            )
        )
    up = [(i, (i + 1) % peers) for i in range(peers)]
    down = [(j, i) for i, j in up]
    beyond = jnp.stack([lax.ppermute(ends[0], "lon", up), lax.ppermute(ends[1], "lon", down)], 1)
    halo_cot = beyond[: 5 * levels].reshape(5, levels, 2, lat)
    halo_vw = beyond[5 * levels : 6 * levels]
    halo_zc = beyond[6 * levels :]
    halo_adj = adjoint_part(halo_cot, halo_vw)

    smoothed = polar_filter(grouped, cutoff, peers)
    smoothed = smoothed.reshape(peers, 5, levels, rows, lon_dev + 2)
    smoothed = smoothed.transpose(1, 2, 4, 0, 3).reshape(5, levels, lon_dev + 2, 2 * POLAR)
    inner = smoothed[:, :, 1 : lon_dev + 1]
    gap = jnp.zeros((5, levels, lon_dev, 256 - 2 * POLAR), jnp.float32)
    smooth = jnp.concatenate([inner[..., :POLAR], gap, inner[..., POLAR:]], 3)
    outer = smoothed[:, :, :: lon_dev + 1]
    halo_f = jnp.concatenate([outer[..., :POLAR], halo_adj[..., POLAR : lat - POLAR], outer[..., POLAR:]], 3)
    halo = jnp.stack(coupled(halo_zc, [halo_f[f] for f in range(5)], 0))

    tail = later_sum(cotangent[2].sum(0))
    first = vertical_wind[0][None] * cotangent[:, 0]
    last = vertical_wind[-1][None] * cotangent[:, -1]
    common = (cotangent, vertical_wind, zonal_coef, merid_coef, tail, smooth, halo)
    if count == 2 and levels > 1:
        got = lax.ppermute(jnp.where(seat == 0, last, first), "lev", [(0, 1), (1, 0)])
        ids = jnp.arange(levels - 1, dtype=jnp.int32) + seat
        flags = jnp.stack([(ids < levels - 1), (ids > 0)]).astype(jnp.float32)
        part = stencil(ids, flags, *common, (), None)
        ids = jnp.where(seat == 0, levels - 1, 0).astype(jnp.int32)[None]
        sign = jnp.where(seat == 0, 1.0, -1.0)[None]
        flags = jnp.stack([(ids < levels - 1), (ids > 0)]).astype(jnp.float32)
        flags = jnp.concatenate([flags, sign[None]], 0)
        return stencil(ids, flags, *common, (got,), part)
    above, under = swap_levels(first, last)
    ids = jnp.arange(levels, dtype=jnp.int32)
    flags = jnp.stack(
        [ids < levels - 1, ids > 0, ids == levels - 1, ids == 0]
    ).astype(jnp.float32) * jnp.array([1.0, 1.0, 1.0, -1.0], jnp.float32)[:, None]
    return stencil(ids, flags, *common, (above, under), None)


def solution(mesh):
    return jax.shard_map(
        body,
        mesh=mesh,
        in_specs=(
            P(None, "lev", "lon", None),
            P("lev", "lon", None),
            P("lev", "lon", None),
            P("lev", "lon", None),
            P(),
        ),
        out_specs=P(None, "lev", "lon", None),
        check_vma=False,
    )
```

time: 1770 us -> 359 us (0.20)
  matrix products: 777 us -> 0 us
  blocking collectives: 447 us -> 0 us
  local copies, waits for them, and re-layouts: 248 us -> 110 us
  Pallas kernels: 0 us -> 122 us
  other arithmetic: 155 us -> 35.1 us
  waiting for transfers between devices: 109 us -> 76.9 us
    dot_general x1 -> x0, matrix products: 777 us -> none  [body(): jnp.einsum('fapj,lpj->falj', piece, kernel, precision=lax.Precision.HIGHEST)]
    all_to_all x2 -> x0, blocking collectives: 447 us -> none  [the longest x1 278 us: body(): lax.all_to_all(packed, 'lev', split_axis=3, concat_axis=1, tiled=True)]
    pallas_call x0 -> x3, Pallas kernels: none -> 122 us  [the longest x1 83.9 us: polar_filter(): pl.pallas_call(functools.partial(filter_kernel, peers), out_shape=jax.Sha...]
    all_gather x1 -> x0, waiting for transfers between devices: 109 us -> none  [body(): piece = lax.all_gather(polar_rows, 'lon', axis=2, tiled=True)]
    ppermute x2 -> x8, waiting for transfers between devices: 0.01 us -> 76.9 us  [the longest x2 74.9 us: swap_levels(): lax.ppermute(jnp.where(seat == 0, last, first), 'lev', [(0, 1), (1, 0)])]
    all_to_all x3 -> x0, local copies, waits for them, and re-layouts: 61 us -> none  [the longest x2 34.8 us: body(): lax.all_to_all(updated, 'lev', split_axis=1, concat_axis=3, tiled=True)]
    add x5 -> x3, other arithmetic: 56.8 us -> 2 us  [the longest x2 1.46 us: adjoint_part(): return (cot + (above - under)).at[3].add(-COUPLE_B * below)]
    mul x4 -> x3, other arithmetic: 44.6 us -> 0.14 us  [the longest x2 0.14 us: adjoint_part(): weighted = vw[None] * cot]
  transfers between devices with their start and end apart: 3 -> 8, of which waited for: 1 -> 2; matrix products, arithmetic and copies ran while one was open for 4% -> 36% of each run, Pallas kernels for 0% -> 31%
where the time goes in v1:
time: 359 us; the launch traced here: 355 us
  Pallas kernels  122 us (34%)
  local copies, waits for them, and re-layouts  110 us (31%)
  waiting for transfers between devices  76.9 us (21%)
  other arithmetic  35.1 us (10%)
  starting transfers between devices  10.2 us (3%)
    pallas_call x1, Pallas kernels, polar_filter(): pl.pallas_call(functools.partial(filter_kernel, peers), out_shape=jax.Sha...  83.9 us
    ppermute x2, waiting for transfers between devices, swap_levels(): lax.ppermute(jnp.where(seat == 0, last, first), 'lev', [(0, 1), (1, 0)])  74.9 us
    unnamed x58, local copies, waits for them, and re-layouts  52.3 us
    pallas_call x2, Pallas kernels, stencil(): pl.pallas_call(functools.partial(stencil_kernel, tiles, levels, len(edges...  38.5 us
    slice x1, local copies, waits for them, and re-layouts, body(): last = vertical_wind[-1][None] * cotangent[:, -1]  16.8 us
    pallas_call x1, local copies, waits for them, and re-layouts, stencil(): pl.pallas_call(functools.partial(stencil_kernel, tiles, levels, len(edges...  12.6 us
  transfers between devices with their start and end apart: 8, of which 2 were waited for; matrix products, arithmetic and copies ran while one was open for 36% of the time, Pallas kernels for 31%

profile of v1, /device:TPU:27, one launch (start us, length us, event | category | flops | bytes accessed | tf_op | source)
XLA Modules:
  0.0 355.1 jit_solution(4009316898832050832)
XLA Ops:
  3.8 4.1 %slice_reduce_fusion = f32[180,1024]{1,0:T(8,128)} fusion(f32[5,4,180,1024]{3,1,2,0:T(4,128)} %param.9), kind=kLoop, calls=%fused_computation.6 | loop fusion | flops 552960 | bytes 3686400 | tf_op jit(solution)/shard_map/reduce_sum | solution.py:337
  10.5 4.4 %fusion.47 = (f32[5,4,180,32]{3,1,2,0:T(4,128)}, f32[5,4,180,32]{3,1,2,0:T(4,128)S(1)}) fusion(f32[5,4,180,1024]{3,1,2,0:T(4,128)} %param.9), kind=kLoop, calls=%fused_computation.107 | loop fusion | bytes 1843200 | tf_op jit(solution)/shard_map/slice | solution.py:296
  15.4 2.3 copy.104
  17.7 1.8 copy.105
  20.6 3.0 collective-permute-start.1
  26.9 2.0 fusion.16
  29.0 3.6 %copy.100.vw = f32[4,180,1024]{2,1,0:T(8,128)S(1)} copy(f32[4,180,1024]{2,0,1:T(4,128)} %param.12) | data formatting | bytes 5898240 | tf_op args[3]
  34.4 16.8 %fusion.45 = (f32[5,1,180,1024]{3,1,2,0:T(1,128)}, f32[5,1,180,1024]{3,1,2,0:T(1,128)}) fusion(f32[5,4,180,1024]{3,1,2,0:T(4,128)} %param.9), kind=kLoop, calls=%fused_computation.105 | loop fusion | bytes 14745600 | tf_op jit(solution)/shard_map/slice | solution.py:339
  52.6 2.7 fusion.9
  58.6 1.9 pad_maximum_fusion.2.fwd_ref
  60.6 7.2 %fusion.1 = f32[5,180,1024]{2,1,0:T(8,128)} fusion(f32[5,1,180,1024]{3,1,2,0:T(1,128)} %get-tuple-element.34, f32[5,1,180,1024]{3,1,2,0:T(1,128)} %get-tuple-element.33, f32[180,1024]{1,0:T(8,128)S(1)} %copy-done.13, f32[180,1024]{1,0:T(8,128)S(1)} %copy-done.12, pred[]{:T(512)S(6)} %eq.31), kind=kLoop, calls=%fused_computation.3 | loop fusion | flops 2764800 | bytes 12533761 | tf_op jit(solution)/shard_map/jit(_where)/select_n | solution.py:342
  67.8 3.4 copy.101.zc
  71.2 29.3 %copy.99.cot = f32[5,4,180,1024]{3,2,1,0:T(8,128)} copy(f32[5,4,180,1024]{3,1,2,0:T(4,128)} %param.9) | data formatting | bytes 29491200 | tf_op args[0]
  101.2 5.2 %copy.102.mc = f32[4,180,1024]{2,1,0:T(8,128)} copy(f32[4,180,1024]{2,0,1:T(4,128)} %param.11) | data formatting | bytes 5898240 | tf_op args[2]
  107.7 2.7 collective-permute-start.7
  115.9 74.9 %collective-permute-done.5 = f32[5,2,1024]{2,1,0:T(2,128)S(1)} collective-permute-done((f32[5,2,1024]{2,1,0:T(2,128)}, f32[5,2,1024]{2,1,0:T(2,128)S(1)}, u32[]{:S(2)}, u32[]{:S(2)}) %collective-permute-start.5) | collective-permute-done | bytes 40992 | tf_op jit(solution)/shard_map/ppermute | solution.py:271
  193.2 2.0 collective-permute-done.6
  204.5 83.9 %polar_filter.1 = f32[16,80,182]{2,1,0:T(8,128)S(1)} custom-call(f32[16,80,180]{2,1,0:T(8,128)S(1)} %reshape.388.x_ref, f32[180,768]{1,0:T(8,128)S(1)} %copy-done, f32[2,384,182]{2,1,0:T(8,128)S(1)} %pad_maximum_fusion.1.inv_ref, f32[16,1,384]{2,1,0:T(1,128)S(1)} %copy-done.1, f32[16,1,384]{2,1,0:T(1,128)S(1)} %get-tuple-element.62.st_ref, ...), custom_call_target="tpu_custom_call" | custom-call | flops 8000000000 | bytes 60000000 | tf_op jit(solution)/shard_map/polar_filter/pallas_call | solution.py:130
  291.7 2.9 slice.198
  297.3 1.9 copy.107
  299.8 4.1 %pad_maximum_fusion.smooth = f32[5,4,180,256]{3,2,1,0:T(8,128)} fusion(f32[5,4,180,32]{3,2,1,0:T(8,128)} %copy.107, f32[5,4,180,32]{3,2,1,0:T(8,128)S(1)} %copy.106, f32[256]{0:T(256)S(1)} %copy-done.22), kind=kLoop, calls=%fused_computation | loop fusion | flops 1843200 | bytes 4609024 | tf_op jit(solution)/shard_map/concatenate | solution.py:332
  303.9 25.9 %stencil.2.rest_1_ = f32[5,4,180,1024]{3,2,1,0:T(8,128)} custom-call(s32[3]{0:T(128)} %iota_add_fusion.1.ids, f32[2,3]{1,0:T(2,128)} %add_convert_fusion.1.flags, f32[5,4,180,1024]{3,2,1,0:T(8,128)} %copy.99.cot, f32[4,180,1024]{2,1,0:T(8,128)} %copy-done.2, f32[4,180,1024]{2,1,0:T(8,128)} %copy.101.zc, f32[4,180,1024]{2,1,0:T(8,128)} %copy.102.mc, ...), custom_call_target="tpu_custom_call" | custom-call | flops 82944000 | bytes 28753920 | tf_op jit(solution)/shard_map/stencil/pallas_call | solution.py:241
  329.8 12.6 %stencil.3 = f32[5,4,180,1024]{3,2,1,0:T(8,128)} custom-call(s32[1]{0:T(128)} %bitcast.ids, f32[3,1]{1,0:T(4,128)} %copy.98.flags, f32[5,4,180,1024]{3,2,1,0:T(8,128)} %copy.99.cot, f32[4,180,1024]{2,1,0:T(8,128)} %copy-done.2, f32[4,180,1024]{2,1,0:T(8,128)} %copy.101.zc, f32[4,180,1024]{2,1,0:T(8,128)} %copy.102.mc, ...), custom_call_target="tpu_custom_call", output_to_operand_aliasing={{}: (10, {})} | custom-call | flops 27648000 | bytes 9584640 | tf_op jit(solution)/shard_map/stencil/pallas_call | solution.py:241
  342.3 12.6 %copy.103 = f32[5,4,180,1024]{3,1,2,0:T(4,128)} copy(f32[5,4,180,1024]{3,2,1,0:T(8,128)} %stencil.3) | data formatting | bytes 29491200 | tf_op jit(solution)/shard_map/stencil/pallas_call | solution.py:241
  (128 shorter events, 43.2 us)
Async XLA Ops:
  2.4 105.2 %collective-permute-start.3 = (f32[28,1024]{1,0:T(8,128)}, f32[28,1024]{1,0:T(8,128)}, u32[]{:S(2)}, u32[]{:S(2)}) collective-permute-start(f32[28,1024]{1,0:T(8,128)} %pad_maximum_fusion.4), channel_id=1, source_target_pairs={{0,2},{2,4},{4,6},{6,8},{8,10},{10,12},{12,14},{14,16},{16,18},{18... | collective-permute-start | bytes 344072 | tf_op jit(solution)/shard_map/ppermute | solution.py:321
  3.1 108.2 %collective-permute-start.4 = (f32[28,1024]{1,0:T(8,128)}, f32[28,1024]{1,0:T(8,128)}, u32[]{:S(2)}, u32[]{:S(2)}) collective-permute-start(f32[28,1024]{1,0:T(8,128)} %pad_maximum_fusion.5), channel_id=1, source_target_pairs={{2,0},{4,2},{6,4},{8,6},{10,8},{12,10},{14,12},{16,14},{18,16},{20... | collective-permute-start | bytes 344072 | tf_op jit(solution)/shard_map/ppermute | solution.py:321
  7.9 296.0 %collective-permute-start = (f32[180,1024]{1,0:T(8,128)}, f32[180,1024]{1,0:T(8,128)}, u32[]{:S(2)}, u32[]{:S(2)}) collective-permute-start(f32[180,1024]{1,0:T(8,128)} %slice_reduce_fusion), channel_id=1, source_target_pairs={{1,0},{3,2},{5,4},{7,6},{9,8},{11,10},{13,12},{15,14},{17,16},{19,... | collective-permute-start | bytes 2211848 | tf_op jit(solution)/shard_map/ppermute | solution.py:282
  17.7 5.9 %copy-start.5 = (f32[5,4,180,32]{2,3,1,0:T(8,128)}, f32[5,4,180,32]{2,3,1,0:T(8,128)S(1)}, u32[]{:S(2)}) copy-start(f32[5,4,180,32]{2,3,1,0:T(8,128)S(1)} %copy.104) | copy-start | bytes 1382404
  19.5 4.1 %copy-start.7 = (f32[5,4,180,32]{2,3,1,0:T(8,128)}, f32[5,4,180,32]{2,3,1,0:T(8,128)S(1)}, u32[]{:S(2)}) copy-start(f32[5,4,180,32]{2,3,1,0:T(8,128)S(1)} %copy.105) | copy-start | bytes 1382404
  19.7 5.4 %copy-start.3 = (f32[5,4,64,180]{3,2,0,1:T(8,128)}, f32[5,4,64,180]{3,2,0,1:T(8,128)S(1)}, u32[]{:S(2)}) copy-start(f32[5,4,64,180]{3,2,0,1:T(8,128)S(1)} %copy_multiply_fusion) | copy-start | bytes 2764804
  20.6 175.5 %collective-permute-start.1 = (f32[5,64,180]{2,1,0:T(8,128)}, f32[5,64,180]{2,1,0:T(8,128)}, u32[]{:S(2)}, u32[]{:S(2)}) collective-permute-start(f32[5,64,180]{2,1,0:T(8,128)} %fusion.11), channel_id=1, source_target_pairs={{0,1},{1,0},{2,3},{3,2},{4,5},{5,4},{6,7},{7,6},{8,9},{9,8},{10,11... | collective-permute-start | bytes 691208 | tf_op jit(solution)/shard_map/ppermute | solution.py:271
  25.1 172.5 %collective-permute-start.2 = (f32[64,180]{1,0:T(8,128)}, f32[64,180]{1,0:T(8,128)}, u32[]{:S(2)}, u32[]{:S(2)}) collective-permute-start(f32[64,180]{1,0:T(8,128)} %get-tuple-element.49), channel_id=1, source_target_pairs={{1,0},{3,2},{5,4},{7,6},{9,8},{11,10},{13,12},{15,14},{17,16},{19,... | collective-permute-start | bytes 138248 | tf_op jit(solution)/shard_map/ppermute | solution.py:282
  29.0 3.7 %copy-start.4 = (f32[5,4,64,180]{3,2,0,1:T(8,128)S(1)}, f32[5,4,64,180]{3,2,0,1:T(8,128)}, u32[]{:S(2)}) copy-start(f32[5,4,64,180]{3,2,0,1:T(8,128)} %copy-done.3) | copy-start | bytes 2764804
  32.6 22.6 %copy-start.2 = (f32[4,180,1024]{2,1,0:T(8,128)}, f32[4,180,1024]{2,1,0:T(8,128)S(1)}, u32[]{:S(2)}) copy-start(f32[4,180,1024]{2,1,0:T(8,128)S(1)} %copy.100.vw) | copy-start | bytes 8847364
  55.2 3.2 copy-start.23
  56.6 3.9 %copy-start.18 = (f32[1,384,182]{2,1,0:T(8,128)S(1)}, f32[1,384,182]{2,1,0:T(8,128)}, u32[]{:S(2)}) copy-start(f32[1,384,182]{2,1,0:T(8,128)} %get-tuple-element.65) | copy-start | bytes 838660
  56.6 4.0 %copy-start.12 = (f32[180,1024]{1,0:T(8,128)S(1)}, f32[180,1024]{1,0:T(8,128)}, u32[]{:S(2)}) copy-start(f32[180,1024]{1,0:T(8,128)} %get-tuple-element.39) | copy-start | bytes 2211844
  56.6 4.0 %copy-start.13 = (f32[180,1024]{1,0:T(8,128)S(1)}, f32[180,1024]{1,0:T(8,128)}, u32[]{:S(2)}) copy-start(f32[180,1024]{1,0:T(8,128)} %get-tuple-element.40) | copy-start | bytes 2211844
  60.6 7.2 %copy-start.11 = (f32[4,180,1024]{2,0,1:T(4,128)S(1)}, f32[4,180,1024]{2,0,1:T(4,128)}, u32[]{:S(2)}) copy-start(f32[4,180,1024]{2,0,1:T(4,128)} %param.10) | copy-start | bytes 8847364
  107.7 222.1 %collective-permute-start.7 = (f32[5,180,1024]{2,1,0:T(8,128)}, f32[5,180,1024]{2,1,0:T(8,128)}, u32[]{:S(2)}, u32[]{:S(2)}) collective-permute-start(f32[5,180,1024]{2,1,0:T(8,128)} %fusion.1), channel_id=1, source_target_pairs={{0,1},{1,0},{2,3},{3,2},{4,5},{5,4},{6,7},{7,6},{8,9},{9,8},{10,11... | collective-permute-start | bytes 11059208 | tf_op jit(solution)/shard_map/ppermute | solution.py:342
  112.5 84.7 %copy-start.6 = (f32[5,4,180,32]{2,3,1,0:T(8,128)S(1)}, f32[5,4,180,32]{2,3,1,0:T(8,128)}, u32[]{:S(2)}) copy-start(f32[5,4,180,32]{2,3,1,0:T(8,128)} %copy-done.5) | copy-start | bytes 1382404
  112.5 84.7 %copy-start.8 = (f32[5,4,180,32]{2,3,1,0:T(8,128)S(1)}, f32[5,4,180,32]{2,3,1,0:T(8,128)}, u32[]{:S(2)}) copy-start(f32[5,4,180,32]{2,3,1,0:T(8,128)} %copy-done.7) | copy-start | bytes 1382404
  112.5 84.7 %copy-start.9 = (f32[5,3,64,180]{3,2,0,1:T(8,128)S(1)}, f32[5,3,64,180]{3,2,0,1:T(8,128)}, u32[]{:S(2)}) copy-start(f32[5,3,64,180]{3,2,0,1:T(8,128)} %get-tuple-element.51) | copy-start | bytes 2073604
  115.0 82.2 %copy-start.10 = (f32[5,3,64,180]{3,2,0,1:T(8,128)S(1)}, f32[5,3,64,180]{3,2,0,1:T(8,128)}, u32[]{:S(2)}) copy-start(f32[5,3,64,180]{3,2,0,1:T(8,128)} %get-tuple-element.52) | copy-start | bytes 2073604
  115.0 75.8 %collective-permute-start.5 = (f32[5,2,1024]{2,1,0:T(2,128)}, f32[5,2,1024]{2,1,0:T(2,128)S(1)}, u32[]{:S(2)}, u32[]{:S(2)}) collective-permute-start(f32[5,2,1024]{2,1,0:T(2,128)} %fusion.22), channel_id=1, source_target_pairs={{0,1},{1,0},{2,3},{3,2},{4,5},{5,4},{6,7},{7,6},{8,9},{9,8},{10,11... | collective-permute-start | bytes 122888 | tf_op jit(solution)/shard_map/ppermute | solution.py:271
  190.8 4.4 %collective-permute-start.6 = (f32[2,1024]{1,0:T(2,128)S(1)}, f32[2,1024]{1,0:T(2,128)S(1)}, u32[]{:S(2)}, u32[]{:S(2)}) collective-permute-start(f32[2,1024]{1,0:T(2,128)S(1)} %get-tuple-element.31), channel_id=1, source_target_pairs={{1,0},{3,2},{5,4},{7,6},{9,8},{11,10},{13,12},{15,14},{17,16},{19,... | collective-permute-start | bytes 24584 | tf_op jit(solution)/shard_map/ppermute | solution.py:282
  297.3 2.4 copy-start.22
  299.7 4.1 %copy-start.20 = (f32[5,4,2,1024]{3,2,1,0:T(2,128)}, f32[5,4,2,1024]{3,2,1,0:T(2,128)S(1)}, u32[]{:S(2)}) copy-start(f32[5,4,2,1024]{3,2,1,0:T(2,128)S(1)} %fusion.26.halo) | copy-start | bytes 491524
  (8 other events, 10.8 us)

commit v2 on v1

v2 whole, which is shorter than its diff:
```python
import functools
import math

import jax
import jax.numpy as jnp
from jax import lax
from jax.experimental import pallas as pl
from jax.experimental.pallas import tpu as pltpu
from jax.sharding import PartitionSpec as P

POLAR = 32
KMAX = 360
COUPLE_G = 0.3
COUPLE_H = 0.3
COUPLE_B = 0.2
MESH = pl.DeviceIdType.MESH
HIGHEST = lax.Precision.HIGHEST


def angles(left, right, period):
    turn = (left * right) % period
    phase = turn.astype(jnp.float32) * (2.0 * math.pi / period)
    return jnp.cos(phase), jnp.sin(phase)


def filter_kernel(
    peers, x_ref, fwd_ref, inv_ref, ct_ref, st_ref, mask_ref, out_ref, held, made,
    own_sem, send_a, recv_a, send_b, recv_b,
):
    me = lax.axis_index("lon")
    kpad = ct_ref.shape[2]
    barrier = pltpu.get_barrier_semaphore()

    def greet(o, _):
        pl.semaphore_signal(
            barrier, inc=1, device_id={"lon": lax.rem(me + o, peers)}, device_id_type=MESH
        )
        return 0

    lax.fori_loop(1, peers, greet, 0)
    pl.semaphore_wait(barrier, peers - 1)

    def out_copy(o):
        d = lax.rem(me + o, peers)
        return pltpu.make_async_remote_copy(
            src_ref=x_ref.at[d], dst_ref=held.at[me], send_sem=send_a.at[d],
            recv_sem=recv_a.at[me], device_id={"lon": d}, device_id_type=MESH,
        )

    def in_copy(o):
        s = lax.rem(me + o, peers)
        return pltpu.make_async_remote_copy(
            src_ref=x_ref.at[s], dst_ref=held.at[s], send_sem=send_a.at[s],
            recv_sem=recv_a.at[s], device_id={"lon": s}, device_id_type=MESH,
        )

    def back_copy(o):
        d = lax.rem(me + o, peers)
        return pltpu.make_async_remote_copy(
            src_ref=made.at[d], dst_ref=out_ref.at[me], send_sem=send_b.at[d],
            recv_sem=recv_b.at[me], device_id={"lon": d}, device_id_type=MESH,
        )

    def home_copy(o):
        s = lax.rem(me + o, peers)
        return pltpu.make_async_remote_copy(
            src_ref=made.at[s], dst_ref=out_ref.at[s], send_sem=send_b.at[s],
            recv_sem=recv_b.at[s], device_id={"lon": s}, device_id_type=MESH,
        )

    lax.fori_loop(1, peers, lambda o, c: (out_copy(o).start(), c)[1], 0)
    own = pltpu.make_async_copy(x_ref.at[me], held.at[me], own_sem)
    own.start()
    own.wait()
    lax.fori_loop(1, peers, lambda o, c: (in_copy(o).wait_recv(), c)[1], 0)

    cols = held.shape[1]
    zero = jnp.zeros((cols, kpad), jnp.float32)

    def gather(s, carry):
        a, b = carry
        both = jnp.dot(held[s], fwd_ref[...], precision=HIGHEST, preferred_element_type=jnp.float32)
        c, v = both[:, :kpad], both[:, kpad:]
        ct, st = ct_ref[s], st_ref[s]
        return a + (ct * c - st * v), b + (st * c + ct * v)

    a, b = lax.fori_loop(0, peers, gather, (zero, zero))
    a = a * mask_ref[...]
    b = b * mask_ref[...]

    def spread(d, carry):
        a, b = carry
        ct, st = ct_ref[d], st_ref[d]
        made[d] = jnp.dot(
            a * ct + b * st, inv_ref[0], precision=HIGHEST, preferred_element_type=jnp.float32
        ) + jnp.dot(
            b * ct - a * st, inv_ref[1], precision=HIGHEST, preferred_element_type=jnp.float32
        )
        return carry

    lax.fori_loop(0, peers, spread, (a, b))
    lax.fori_loop(1, peers, lambda o, c: (back_copy(o).start(), c)[1], 0)
    mine = pltpu.make_async_copy(made.at[me], out_ref.at[me], own_sem)
    mine.start()
    mine.wait()
    lax.fori_loop(1, peers, lambda o, c: (home_copy(o).wait_recv(), c)[1], 0)
    lax.fori_loop(1, peers, lambda o, c: (out_copy(o).wait_send(), c)[1], 0)
    lax.fori_loop(1, peers, lambda o, c: (back_copy(o).wait_send(), c)[1], 0)


def polar_filter(x, cutoff, peers):
    _, cols, lon_dev = x.shape
    nlon = peers * lon_dev
    rows = cutoff.shape[0] // peers
    kpad = (KMAX + 1 + 127) // 128 * 128
    wave = jnp.arange(kpad, dtype=jnp.int32)
    place = jnp.arange(lon_dev, dtype=jnp.int32)
    fwd = jnp.concatenate(angles(place[:, None], wave[None, :], nlon), axis=1)
    wide = jnp.arange(-1, lon_dev + 1, dtype=jnp.int32)
    inv = jnp.stack(angles(wave[:, None], wide[None, :] % nlon, nlon))
    seat = jnp.arange(peers, dtype=jnp.int32) * lon_dev
    ct, st = angles(seat[:, None, None], wave[None, None, :], nlon)
    mine = lax.dynamic_slice_in_dim(cutoff, lax.axis_index("lon") * rows, rows)
    weight = jnp.where(wave == 0, 1.0 / nlon, 2.0 / nlon)
    mask = jnp.where(wave[None, :] <= mine[:, None], weight[None, :], 0.0)
    mask = jnp.tile(mask, (cols // rows, 1))
    vmem = pl.BlockSpec(memory_space=pltpu.VMEM)
    dma = pltpu.SemaphoreType.DMA
    return pl.pallas_call(
        functools.partial(filter_kernel, peers),
        out_shape=jax.ShapeDtypeStruct((peers, cols, lon_dev + 2), jnp.float32),
        in_specs=[vmem] * 6,
        out_specs=vmem,
        scratch_shapes=[
            pltpu.VMEM((peers, cols, lon_dev), jnp.float32),
            pltpu.VMEM((peers, cols, lon_dev + 2), jnp.float32),
            dma(()), dma((peers,)), dma((peers,)), dma((peers,)), dma((peers,)),
        ],
        compiler_params=pltpu.CompilerParams(
            collective_id=0, has_side_effects=True, vmem_limit_bytes=24 << 20
        ),
        cost_estimate=pl.CostEstimate(flops=8_000_000_000, bytes_accessed=60_000_000, transcendentals=0),
        name="polar_filter",
    )(x, fwd, inv, ct, st, mask)


def to_rows(x):
    *lead, levels, lon, lat = x.shape
    n = len(lead)
    x = x.reshape(*lead, levels, lon, lat // 128, 128)
    x = x.transpose(*range(n), n + 1, n + 2, n, n + 3)
    return x.reshape(*lead, lon, lat // 128 * levels, 128)


def from_rows(x, levels):
    *lead, lon, rows, _ = x.shape
    n = len(lead)
    x = x.reshape(*lead, lon, rows // levels, levels, 128)
    x = x.transpose(*range(n), n + 2, n, n + 1, n + 3)
    return x.reshape(*lead, levels, lon, rows // levels * 128)


def chunk_of(lon):
    return max(d for d in range(1, 21) if lon % d == 0)


def edge_kernel(levels, choose, seat, cot, vw, *outs):
    fields, chunk, rows, _ = cot.shape
    tiles = rows // levels
    flat_c = cot.reshape(fields * chunk * rows, 128)
    flat_v = vw.reshape(chunk * rows, 128)
    *sends, tail = outs

    def level(ref, count, k):
        return ref[pl.ds(k, count * tiles, stride=levels), :] if levels > 1 else ref[...]

    def product(k, sign, out):
        c = level(flat_c, fields * chunk, k).reshape(fields, chunk, tiles, 128)
        v = level(flat_v, chunk, k).reshape(1, chunk, tiles, 128)
        out[...] = sign * (v * c)

    if choose:
        pl.when(seat[0] == 0)(lambda: product(levels - 1, -1.0, sends[0]))
        pl.when(seat[0] != 0)(lambda: product(0, 1.0, sends[0]))
    else:
        product(0, 1.0, sends[0])
        product(levels - 1, -1.0, sends[1])
    flat_t = cot.at[2].reshape(chunk * rows, 128)
    total = level(flat_t, chunk, 0)
    for k in range(1, levels):
        total = total + level(flat_t, chunk, k)
    tail[...] = total.reshape(chunk, tiles, 128)


def edges_of(seat, cot, vw, levels, choose):
    fields, lon, rows, _ = cot.shape
    tiles = rows // levels
    chunk = chunk_of(lon)
    n = 1 if choose else 2
    return pl.pallas_call(
        functools.partial(edge_kernel, levels, choose),
        out_shape=[jax.ShapeDtypeStruct((fields, lon, tiles, 128), jnp.float32)] * n
        + [jax.ShapeDtypeStruct((lon, tiles, 128), jnp.float32)],
        grid_spec=pltpu.PrefetchScalarGridSpec(
            num_scalar_prefetch=1,
            grid=(lon // chunk,),
            in_specs=[
                pl.BlockSpec((fields, chunk, rows, 128), lambda g, s: (0, g, 0, 0)),
                pl.BlockSpec((chunk, rows, 128), lambda g, s: (g, 0, 0)),
            ],
            out_specs=[pl.BlockSpec((fields, chunk, tiles, 128), lambda g, s: (0, g, 0, 0))] * n
            + [pl.BlockSpec((chunk, tiles, 128), lambda g, s: (g, 0, 0))],
        ),
        compiler_params=pltpu.CompilerParams(vmem_limit_bytes=24 << 20),
        cost_estimate=pl.CostEstimate(flops=10_000_000, bytes_accessed=22_000_000, transcendentals=0),
        name="edges",
    )(seat, cot, vw)


def coupled(coef, fields, first):
    flux = [coef * f for f in fields]
    flux[first] = flux[first] + COUPLE_H * fields[3]
    flux[3] = flux[3] + COUPLE_G * fields[first]
    return flux


def stencil_kernel(levels, steps, n_edge, seat, cot, vw, zc, mc, tail, smooth, halo, *rest):
    edges = rest[:n_edge]
    out, ready, final, wait, prior, spread, below_ref, sems, last_sem = rest[n_edge:]
    _, chunk, rows, _ = cot.shape
    tiles = rows // levels
    g = pl.program_id(0)
    slot = lax.rem(g, 2)
    lane = lax.broadcasted_iota(jnp.int32, (rows, 128), 1)
    row = lax.broadcasted_iota(jnp.int32, (rows, 128), 0)
    k = lax.rem(row, levels)
    cap_lane = lax.broadcasted_iota(jnp.int32, (2 * levels, 128), 1)
    cap_row = lax.broadcasted_iota(jnp.int32, (2 * levels, 128), 0)
    north = (cap_row < levels) & (cap_lane < POLAR)
    south = (cap_row >= levels) & (cap_lane >= 128 - POLAR)

    def first_copy():
        return pltpu.make_async_copy(
            ready.at[0, :, pl.ds(1, chunk - 1)], out.at[:, pl.ds(0, chunk - 1)], sems.at[0]
        )

    def copy(at):
        s = lax.rem(at, 2)
        return pltpu.make_async_copy(
            ready.at[s], out.at[:, pl.ds(at * chunk - 1, chunk)], sems.at[s]
        )

    @pl.when(g == 0)
    def _():
        spread[...] = jnp.zeros_like(spread)
        for f in range(5):
            prior[f] = halo[f, 0]
            wait[f] = jnp.zeros((rows, 128), jnp.float32)

    pl.when(g == 2)(lambda: first_copy().wait())
    pl.when(g > 2)(lambda: copy(g - 2).wait())

    def put(ref, at, value):
        if levels > 1:
            ref[pl.ds(at, tiles, stride=levels), :] = value
        else:
            ref[...] = value

    def one(l, _):
        for f in range(5):
            if n_edge == 1:
                pl.when(seat[0] == 0)(lambda: put(spread.at[0, f], levels - 1, edges[0][f, l]))
                pl.when(seat[0] != 0)(lambda: put(spread.at[0, f], 0, edges[0][f, l]))
            else:
                put(spread.at[0, f], levels - 1, edges[0][f, l])
                put(spread.at[1, f], 0, edges[1][f, l])
        for at in range(levels):
            put(below_ref, at, tail[l])
        wind = vw[l]
        base, fields = [], []
        for f in range(5):
            c = cot[f, l]
            w = wind * c
            a = c
            if levels > 1:
                up = jnp.where(k < levels - 1, pltpu.roll(w, rows - 1, 0), 0.0)
                a = a + (up - jnp.where(k > 0, pltpu.roll(w, 1, 0), 0.0))
            for n in range(n_edge):
                a = a + spread[n, f]
            if f == 3:
                theta = cot[2, l]
                below = below_ref[...] + theta
                for r in range(1, levels):
                    below = below + jnp.where(k < levels - r, pltpu.roll(theta, rows - r, 0), 0.0)
                a = a - COUPLE_B * below
            base.append(a)
            s = smooth[f, l]
            top = jnp.where(north, s, a[: 2 * levels])
            low = jnp.where(south, s, a[rows - 2 * levels :])
            fields.append(jnp.concatenate([top, a[2 * levels : rows - 2 * levels], low], 0))
        zonal = coupled(zc[l], fields, 0)
        merid = coupled(mc[l], fields, 1)
        for f in range(5):
            ready[slot, f, l] = wait[f] + zonal[f]
            left = pltpu.roll(merid[f], 1, 1)
            over = jnp.where(row < levels, 0.0, pltpu.roll(left, levels, 0))
            left = jnp.where(lane == 0, over, left)
            right = pltpu.roll(merid[f], 127, 1)
            over = jnp.where(row >= rows - levels, 0.0, pltpu.roll(right, rows - levels, 0))
            right = jnp.where(lane == 127, over, right)
            wait[f] = base[f] + (right - left) - prior[f]
            prior[f] = zonal[f]
        return 0

    lax.fori_loop(0, chunk, one, 0)
    pl.when(g == 0)(lambda: first_copy().start())
    pl.when(g > 0)(lambda: copy(g).start())

    @pl.when(g == steps - 1)
    def _():
        for f in range(5):
            final[f, 0] = wait[f] + halo[f, 1]
        end = pltpu.make_async_copy(final, out.at[:, pl.ds(steps * chunk - 1, 1)], last_sem)
        end.start()
        copy(g - 1).wait() if steps > 2 else first_copy().wait()
        copy(g).wait()
        end.wait()


def stencil(seat, cot, vw, zc, mc, tail, smooth, halo, edges, levels):
    _, lon, rows, _ = cot.shape
    tiles = rows // levels
    chunk = chunk_of(lon)
    steps = lon // chunk
    field = lambda n: pl.BlockSpec((5, chunk, n, 128), lambda g, s: (0, g, 0, 0))
    plain = lambda n: pl.BlockSpec((chunk, n, 128), lambda g, s: (g, 0, 0))
    return pl.pallas_call(
        functools.partial(stencil_kernel, levels, steps, len(edges)),
        out_shape=jax.ShapeDtypeStruct(cot.shape, jnp.float32),
        grid_spec=pltpu.PrefetchScalarGridSpec(
            num_scalar_prefetch=1,
            grid=(steps,),
            in_specs=[field(rows), plain(rows), plain(rows), plain(rows), plain(tiles), field(2 * levels),
                      pl.BlockSpec((5, 2, rows, 128), lambda g, s: (0, 0, 0, 0))]
            + [field(tiles)] * len(edges),
            out_specs=pl.BlockSpec(memory_space=pl.ANY),
            scratch_shapes=[
                pltpu.VMEM((2, 5, chunk, rows, 128), jnp.float32),
                pltpu.VMEM((5, 1, rows, 128), jnp.float32),
                pltpu.VMEM((5, rows, 128), jnp.float32),
                pltpu.VMEM((5, rows, 128), jnp.float32),
                pltpu.VMEM((len(edges), 5, rows, 128), jnp.float32),
                pltpu.VMEM((rows, 128), jnp.float32),
                pltpu.SemaphoreType.DMA((2,)),
                pltpu.SemaphoreType.DMA(()),
            ],
        ),
        compiler_params=pltpu.CompilerParams(vmem_limit_bytes=40 << 20),
        cost_estimate=pl.CostEstimate(
            flops=30 * 5 * lon * rows * 128, bytes_accessed=4 * 14 * lon * rows * 128, transcendentals=0
        ),
        name="stencil",
    )(seat, cot, vw, zc, mc, tail, smooth, halo, *edges)


def swap_levels(first, last):
    count = lax.axis_size("lev")
    if count == 2:
        seat = lax.axis_index("lev")
        got = lax.ppermute(jnp.where(seat == 0, last, first), "lev", [(0, 1), (1, 0)])
        return jnp.where(seat == 0, got, 0.0), jnp.where(seat == 1, got, 0.0)
    up = lax.ppermute(first, "lev", [(i + 1, i) for i in range(count - 1)])
    down = lax.ppermute(last, "lev", [(i, i + 1) for i in range(count - 1)])
    return up, down


def later_sum(local):
    count = lax.axis_size("lev")
    total = jnp.zeros_like(local)
    for r in range(1, count):
        total = total + lax.ppermute(local, "lev", [(i + r, i) for i in range(count - r)])
    return total


def adjoint_part(cot, vw):
    weighted = vw[None] * cot
    up, down = swap_levels(weighted[:, 0], weighted[:, -1])
    above = jnp.concatenate([weighted[:, 1:], up[:, None]], 1)
    under = jnp.concatenate([down[:, None], weighted[:, :-1]], 1)
    below = jnp.flip(jnp.cumsum(jnp.flip(cot[2], 0), 0), 0) + later_sum(cot[2].sum(0))[None]
    return (cot + (above - under)).at[3].add(-COUPLE_B * below)


def polar_cut(x):
    return jnp.concatenate([x[..., :POLAR], x[..., x.shape[-1] - POLAR :]], -1)


def body(cotangent, zonal_coef, merid_coef, vertical_wind, cutoff):
    levels, lon_dev, lat = cotangent.shape[1:]
    peers = lax.axis_size("lon")
    count = lax.axis_size("lev")
    seat = lax.axis_index("lev").astype(jnp.int32)[None]
    cot, vw = to_rows(cotangent), to_rows(vertical_wind)
    *sends, local = edges_of(seat, cot, vw, levels, count == 2)

    polar_cot = jnp.swapaxes(polar_cut(cotangent), 2, 3)
    polar_vw = jnp.swapaxes(polar_cut(vertical_wind), 1, 2)
    polar = adjoint_part(polar_cot, polar_vw)
    ends_adj = adjoint_part(cotangent[:, :, :: lon_dev - 1], vertical_wind[:, :: lon_dev - 1])

    polar, ends_adj, local, *sends = lax.optimization_barrier((polar, ends_adj, local, *sends))
    if count == 2:
        edges = [lax.ppermute(sends[0], "lev", [(0, 1), (1, 0)])]
    else:
        edges = [
            lax.ppermute(sends[0], "lev", [(i + 1, i) for i in range(count - 1)]),
            lax.ppermute(sends[1], "lev", [(i, i + 1) for i in range(count - 1)]),
        ]
    tail = later_sum(local)

    rows = 2 * POLAR // peers
    grouped = polar.reshape(5 * levels, peers, rows, lon_dev)
    grouped = jnp.swapaxes(grouped, 0, 1).reshape(peers, 5 * levels * rows, lon_dev)

    pack = jnp.concatenate([ends_adj.reshape(5 * levels, 2, lat), zonal_coef[:, :: lon_dev - 1]], 0)
    up = [(i, (i + 1) % peers) for i in range(peers)]
    down = [(j, i) for i, j in up]
    beyond = jnp.stack([lax.ppermute(pack[:, 1], "lon", up), lax.ppermute(pack[:, 0], "lon", down)], 1)
    halo_adj = beyond[: 5 * levels].reshape(5, levels, 2, lat)
    halo_zc = beyond[5 * levels :]

    smoothed = polar_filter(grouped, cutoff, peers)
    smoothed = smoothed.reshape(2, peers // 2, 5, levels, rows, lon_dev + 2)
    smoothed = smoothed.transpose(2, 5, 0, 3, 1, 4).reshape(5, lon_dev + 2, 2, levels, POLAR)
    north, south = smoothed[:, :, 0], smoothed[:, :, 1]
    gap = ((0, 0), (0, 0), (0, 0))
    smooth = jnp.concatenate(
        [jnp.pad(north, (*gap, (0, 128 - POLAR))), jnp.pad(south, (*gap, (128 - POLAR, 0)))], 2
    )[:, 1 : lon_dev + 1]
    outer = [jnp.swapaxes(x[:, :: lon_dev + 1], 1, 2) for x in (north, south)]
    halo_f = jnp.concatenate([outer[0], halo_adj[..., POLAR : lat - POLAR], outer[1]], 3)
    halo = jnp.stack(coupled(halo_zc, [halo_f[f] for f in range(5)], 0))
    out = stencil(
        seat, cot, vw, to_rows(zonal_coef), to_rows(merid_coef), tail, smooth, to_rows(halo), edges, levels
    )
    return from_rows(out, levels)


def solution(mesh):
    return jax.shard_map(
        body,
        mesh=mesh,
        in_specs=(
            P(None, "lev", "lon", None),
            P("lev", "lon", None),
            P("lev", "lon", None),
            P("lev", "lon", None),
            P(),
        ),
        out_specs=P(None, "lev", "lon", None),
        check_vma=False,
    )
```

time: 359 us -> 241 us (0.67)
  waiting for transfers between devices: 76.9 us -> 16.2 us
  local copies, waits for them, and re-layouts: 110 us -> 59.4 us
  other arithmetic: 35.1 us -> 24.4 us
    ppermute x2, waiting for transfers between devices: 74.9 us -> 0.01 us  [swap_levels(): lax.ppermute(jnp.where(seat == 0, last, first), 'lev', [(0, 1), (1, 0)])]
    unnamed x58 -> x53, local copies, waits for them, and re-layouts: 52.3 us -> 24.3 us
    slice x5 -> x4, local copies, waits for them, and re-layouts: 21.4 us -> 3.02 us  [the longest x1 1.37 us: body(): north, south = (smoothed[:, :, 0], smoothed[:, :, 1])]
    ppermute x3, waiting for transfers between devices: 1.99 us -> 16.2 us  [later_sum(): lax.ppermute(local, 'lev', [(i + r, i) for i in range(count - r)])]
    pallas_call x1 -> x0, local copies, waits for them, and re-layouts: 12.6 us -> none  [stencil(): pl.pallas_call(functools.partial(stencil_kernel, tiles, levels, len(edges...]
    pallas_call x2, Pallas kernels: 38.5 us -> 46.7 us  [the longest x1 41.9 us: stencil(): pl.pallas_call(functools.partial(stencil_kernel, levels, steps, len(edges...]
    select_n x1 -> x0, other arithmetic: 7.16 us -> none  [body(): jnp.where(seat == 0, last, first)]
    pallas_call x1, Pallas kernels: 83.9 us -> 78.6 us  [polar_filter(): pl.pallas_call(functools.partial(filter_kernel, peers), out_shape=jax.Sha...]
  transfers between devices with their start and end apart: 8 -> 8, of which waited for: 2 -> 1; matrix products, arithmetic and copies ran while one was open for 36% -> 29% of each run, Pallas kernels for 31% -> 35%
where the time goes in v2:
time: 241 us; the launch traced here: 240 us
  Pallas kernels  125 us (52%)
  local copies, waits for them, and re-layouts  59.4 us (25%)
  other arithmetic  24.4 us (10%)
  waiting for transfers between devices  16.2 us (7%)
  starting transfers between devices  13.7 us (6%)
    pallas_call x1, Pallas kernels, polar_filter(): pl.pallas_call(functools.partial(filter_kernel, peers), out_shape=jax.Sha...  78.6 us
    pallas_call x1, Pallas kernels, stencil(): pl.pallas_call(functools.partial(stencil_kernel, levels, steps, len(edges...  41.9 us
    unnamed x53, local copies, waits for them, and re-layouts  24.3 us
    ppermute x3, waiting for transfers between devices, later_sum(): lax.ppermute(local, 'lev', [(i + r, i) for i in range(count - r)])  16.2 us
    slice x2, local copies, waits for them, and re-layouts, polar_cut(): return jnp.concatenate([x[..., :POLAR], x[..., x.shape[-1] - POLAR:]], -1)  6.32 us
  transfers between devices with their start and end apart: 8, of which 1 were waited for; matrix products, arithmetic and copies ran while one was open for 29% of the time, Pallas kernels for 35%

profile of v2, /device:TPU:27, one launch (start us, length us, event | category | flops | bytes accessed | tf_op | source)
XLA Modules:
  0.0 239.6 jit_solution(15372885920212262098)
XLA Ops:
  4.4 2.7 %collective-permute-start.2 = (f32[5,2,1024]{2,1,0:T(2,128)}, f32[5,2,1024]{2,1,0:T(2,128)}, u32[]{:S(2)}, u32[]{:S(2)}) collective-permute-start(f32[5,2,1024]{2,1,0:T(2,128)} %bitcast.130), channel_id=1, source_target_pairs={{0,1},{1,0},{2,3},{3,2},{4,5},{5,4},{6,7},{7,6},{8,9},{9,8},{10,11... | collective-permute-start | bytes 122888 | tf_op jit(solution)/shard_map/ppermute | solution.py:370
  8.4 5.0 %fusion.39 = (f32[5,4,180,32]{3,1,2,0:T(4,128)}, f32[5,4,180,32]{3,1,2,0:T(4,128)}) fusion(f32[5,4,180,1024]{3,1,2,0:T(4,128)} %param.9), kind=kLoop, calls=%fused_computation.92 | loop fusion | bytes 1843200 | tf_op jit(solution)/shard_map/slice | solution.py:395
  13.8 2.3 copy.76
  16.1 2.6 %copy.77 = f32[5,4,180,32]{2,3,1,0:T(8,128)S(1)} copy(f32[5,4,180,32]{3,1,2,0:T(4,128)} %get-tuple-element.46) | data formatting | bytes 921600
  22.5 2.0 fusion.14
  26.1 2.4 %fusion.7 = (f32[1,384,182]{2,1,0:T(8,128)S(1)}, f32[1,384,182]{2,1,0:T(8,128)}) fusion(s32[182]{0:T(256)S(1)} %and_select_fusion), kind=kLoop, calls=%fused_computation.19 | loop fusion | flops 628992 | bytes 559832 | tf_op jit(solution)/shard_map/cos | solution.py:23
  29.4 2.1 pad_maximum_fusion.inv_ref
  36.2 2.5 %rev.16 = f32[4,2,1024]{2,0,1:T(4,128)} reverse(f32[4,2,1024]{2,0,1:T(4,128)S(1)} %get-tuple-element.60), dimensions={0} | reverse | bytes 65536 | tf_op jit(solution)/shard_map/jit(_flip)/rev | solution.py:390
  40.1 2.8 %rev.17 = f32[4,2,1024]{2,0,1:T(4,128)S(1)} reverse(f32[4,2,1024]{2,0,1:T(4,128)} %reduce_window_sum.23), dimensions={0} | reverse | bytes 65536 | tf_op jit(solution)/shard_map/jit(_flip)/rev | solution.py:390
  42.9 5.2 %copy-done = f32[5,4,180,1024]{3,1,2,0:T(4,128)S(1)} copy-done((f32[5,4,180,1024]{3,1,2,0:T(4,128)S(1)}, f32[5,4,180,1024]{3,1,2,0:T(4,128)}, u32[]{:S(2)}) %copy-start) | copy-done | bytes 14745624
  48.1 4.8 %edges.1 = (f32[5,180,8,128]{3,2,1,0:T(8,128)}, f32[180,8,128]{2,1,0:T(8,128)S(1)}) custom-call(s32[1]{0:T(128)} %bitcast.seat, f32[5,180,32,128]{3,2,1,0:T(8,128)S(1)} %bitcast.132, f32[180,32,128]{2,1,0:T(8,128)S(1)} %bitcast.133), custom_call_target="tpu_custom_call" | custom-call | flops 10000000 | bytes 22000000 | tf_op jit(solution)/shard_map/edges/pallas_call | solution.py:200
  57.9 2.8 %collective-permute-start.7 = (f32[5,180,8,128]{3,2,1,0:T(8,128)}, f32[5,180,8,128]{3,2,1,0:T(8,128)}, u32[]{:S(2)}, u32[]{:S(2)}) collective-permute-start(f32[5,180,8,128]{3,2,1,0:T(8,128)} %get-tuple-element.40), channel_id=1, source_target_pairs={{0,1},{1,0},{2,3},{3,2},{4,5},{5,4},{6,7},{7,6},{8,9},{9,8},{10,11... | collective-permute-start | bytes 11059208 | tf_op jit(solution)/shard_map/ppermute | solution.py:413
  63.6 1.8 collective-permute-start.6
  65.4 2.6 %collective-permute-start.5 = (f32[24,1024]{1,0:T(8,128)}, f32[24,1024]{1,0:T(8,128)}, u32[]{:S(2)}, u32[]{:S(2)}) collective-permute-start(f32[24,1024]{1,0:T(8,128)} %bitcast.128), channel_id=1, source_target_pairs={{0,2},{2,4},{4,6},{6,8},{8,10},{10,12},{12,14},{14,16},{16,18},{18... | collective-permute-start | bytes 294920 | tf_op jit(solution)/shard_map/ppermute | solution.py:428
  69.3 2.6 %reshape.390 = f32[20,16,4,180]{3,2,1,0:T(4,128)} reshape(f32[5,4,64,180]{3,2,1,0:T(8,128)} %copy.57) | data formatting | bytes 1843200 | tf_op jit(solution)/shard_map/reshape | solution.py:422
  71.9 2.8 %copy.58 = f32[16,20,4,180]{3,2,1,0:T(4,128)} copy(f32[16,20,4,180]{3,2,0,1:T(4,128)} %bitcast.143) | data formatting | bytes 1843200 | tf_op jit(solution)/shard_map/transpose | solution.py:423
  74.7 2.7 %reshape.391.x_ref = f32[16,80,180]{2,1,0:T(8,128)} reshape(f32[16,20,4,180]{3,2,1,0:T(4,128)} %copy.58) | data formatting | bytes 1843200 | tf_op jit(solution)/shard_map/reshape | solution.py:423
  81.4 78.6 %polar_filter.1 = f32[16,80,182]{2,1,0:T(8,128)S(1)} custom-call(f32[16,80,180]{2,1,0:T(8,128)S(1)} %copy-done.4, f32[180,768]{1,0:T(8,128)S(1)} %pad_maximum_fusion.1.fwd_ref, f32[2,384,182]{2,1,0:T(8,128)S(1)} %copy-done.6, f32[16,1,384]{2,1,0:T(1,128)S(1)} %copy-done.8, f32[16,1,384]{2,1,0:T(1,128)S(1)} %get-tuple-element.65.st_ref, f32[80,384]{1,0:T(8,128)S(1)} %copy-done.7), custom_call_target="tpu_custom_call" | custom-call | flops 8000000000 | bytes 60000000 | tf_op jit(solution)/shard_map/polar_filter/pallas_call | solution.py:129
  161.1 2.7 %reshape.392 = f32[2,8,5,4,4,182]{5,4,3,2,1,0:T(4,128)} reshape(f32[16,80,182]{2,1,0:T(8,128)} %copy-done.5) | data formatting | bytes 1863680 | tf_op jit(solution)/shard_map/reshape | solution.py:433
  166.9 2.9 %copy.79 = f32[5,182,1,4,32]{4,3,1,0,2:T(4,128)} copy(f32[5,182,1,4,32]{1,3,4,2,0:T(4,128)} %get-tuple-element.49) | data formatting | bytes 931840
  169.8 2.9 %copy.80 = f32[5,182,1,4,32]{4,3,1,0,2:T(4,128)} copy(f32[5,182,1,4,32]{1,3,4,2,0:T(4,128)} %get-tuple-element.50) | data formatting | bytes 931840
  174.1 3.4 %fusion.smooth = f32[5,180,8,128]{3,2,1,0:T(8,128)S(1)} fusion(f32[5,182,4,32]{3,2,1,0:T(4,128)} %bitcast.141, f32[5,182,4,32]{3,2,1,0:T(4,128)} %bitcast.139), kind=kLoop, calls=%fused_computation.1 | loop fusion | flops 4608000 | bytes 4618240 | tf_op jit(solution)/shard_map/concatenate | solution.py:437
  181.3 16.2 %collective-permute-done.4.tail = f32[180,8,128]{2,1,0:T(8,128)S(1)} collective-permute-done((f32[180,8,128]{2,1,0:T(8,128)S(1)}, f32[180,8,128]{2,1,0:T(8,128)S(1)}, u32[]{:S(2)}, u32[]{:S(2)}) %collective-permute-start.4) | collective-permute-done | bytes 737312 | tf_op jit(solution)/shard_map/ppermute | solution.py:381
  197.5 41.9 %stencil.1 = f32[5,180,32,128]{3,2,1,0:T(8,128)} custom-call(s32[1]{0:T(128)} %bitcast.seat, f32[5,180,32,128]{3,2,1,0:T(8,128)} %bitcast.131, f32[180,32,128]{2,1,0:T(8,128)S(1)} %bitcast.134, f32[180,32,128]{2,1,0:T(8,128)S(1)} %bitcast.135, f32[180,32,128]{2,1,0:T(8,128)S(1)} %bitcast.136, f32[180,8,128]{2,1,0:T(8,128)S(1)} %collective-permute-done.4.tail, ...), custom_call_target="tpu_custom_call" | custom-call | flops 110592000 | bytes 41287680 | tf_op jit(solution)/shard_map/stencil/pallas_call | solution.py:337
  (110 shorter events, 41.0 us)
Async XLA Ops:
  2.4 51.8 %collective-permute-start.3 = (f32[2,1024]{1,0:T(2,128)}, f32[2,1024]{1,0:T(2,128)}, u32[]{:S(2)}, u32[]{:S(2)}) collective-permute-start(f32[2,1024]{1,0:T(2,128)} %get-tuple-element.59), channel_id=1, source_target_pairs={{1,0},{3,2},{5,4},{7,6},{9,8},{11,10},{13,12},{15,14},{17,16},{19,... | collective-permute-start | bytes 24584 | tf_op jit(solution)/shard_map/ppermute | solution.py:381
  4.4 48.6 %collective-permute-start.2 = (f32[5,2,1024]{2,1,0:T(2,128)}, f32[5,2,1024]{2,1,0:T(2,128)}, u32[]{:S(2)}, u32[]{:S(2)}) collective-permute-start(f32[5,2,1024]{2,1,0:T(2,128)} %bitcast.130), channel_id=1, source_target_pairs={{0,1},{1,0},{2,3},{3,2},{4,5},{5,4},{6,7},{7,6},{8,9},{9,8},{10,11... | collective-permute-start | bytes 122888 | tf_op jit(solution)/shard_map/ppermute | solution.py:370
  16.1 3.5 %copy-start.11 = (f32[5,4,180,32]{2,3,1,0:T(8,128)}, f32[5,4,180,32]{2,3,1,0:T(8,128)S(1)}, u32[]{:S(2)}) copy-start(f32[5,4,180,32]{2,3,1,0:T(8,128)S(1)} %copy.76) | copy-start | bytes 1382404
  19.6 35.3 %collective-permute-start = (f32[5,64,180]{2,1,0:T(8,128)}, f32[5,64,180]{2,1,0:T(8,128)}, u32[]{:S(2)}, u32[]{:S(2)}) collective-permute-start(f32[5,64,180]{2,1,0:T(8,128)} %fusion.9), channel_id=1, source_target_pairs={{0,1},{1,0},{2,3},{3,2},{4,5},{5,4},{6,7},{7,6},{8,9},{9,8},{10,11... | collective-permute-start | bytes 691208 | tf_op jit(solution)/shard_map/ppermute | solution.py:370
  20.4 35.9 %collective-permute-start.1 = (f32[64,180]{1,0:T(8,128)}, f32[64,180]{1,0:T(8,128)}, u32[]{:S(2)}, u32[]{:S(2)}) collective-permute-start(f32[64,180]{1,0:T(8,128)} %get-tuple-element.51), channel_id=1, source_target_pairs={{1,0},{3,2},{5,4},{7,6},{9,8},{11,10},{13,12},{15,14},{17,16},{19,... | collective-permute-start | bytes 138248 | tf_op jit(solution)/shard_map/ppermute | solution.py:381
  26.1 3.2 %copy-start.21 = (s32[64]{0:T(128)S(1)}, s32[64]{0:T(128)}, u32[]{:S(2)}) copy-start(s32[64]{0:T(128)} %param.13) | copy-start | bytes 772
  29.4 13.5 %copy-start.1 = (f32[4,180,1024]{2,0,1:T(4,128)S(1)}, f32[4,180,1024]{2,0,1:T(4,128)}, u32[]{:S(2)}) copy-start(f32[4,180,1024]{2,0,1:T(4,128)} %param.12) | copy-start | bytes 8847364
  42.9 5.2 %copy-start = (f32[5,4,180,1024]{3,1,2,0:T(4,128)S(1)}, f32[5,4,180,1024]{3,1,2,0:T(4,128)}, u32[]{:S(2)}) copy-start(f32[5,4,180,1024]{3,1,2,0:T(4,128)} %param.9) | copy-start | bytes 44236804
  48.1 5.9 %copy-start.18 = (f32[5,3,2,1024]{3,1,2,0:T(4,128)S(1)}, f32[5,3,2,1024]{3,1,2,0:T(4,128)}, u32[]{:S(2)}) copy-start(f32[5,3,2,1024]{3,1,2,0:T(4,128)} %get-tuple-element.61) | copy-start | bytes 368644
  48.1 5.9 %copy-start.19 = (f32[5,3,2,1024]{3,1,2,0:T(4,128)S(1)}, f32[5,3,2,1024]{3,1,2,0:T(4,128)}, u32[]{:S(2)}) copy-start(f32[5,3,2,1024]{3,1,2,0:T(4,128)} %get-tuple-element.62) | copy-start | bytes 368644
  48.1 7.9 %copy-start.15 = (f32[5,3,64,180]{3,2,0,1:T(8,128)S(1)}, f32[5,3,64,180]{3,2,0,1:T(8,128)}, u32[]{:S(2)}) copy-start(f32[5,3,64,180]{3,2,0,1:T(8,128)} %get-tuple-element.53) | copy-start | bytes 2073604
  48.1 7.9 %copy-start.16 = (f32[5,3,64,180]{3,2,0,1:T(8,128)S(1)}, f32[5,3,64,180]{3,2,0,1:T(8,128)}, u32[]{:S(2)}) copy-start(f32[5,3,64,180]{3,2,0,1:T(8,128)} %get-tuple-element.54) | copy-start | bytes 2073604
  52.9 3.4 %copy-start.9 = (f32[180,8,128]{2,1,0:T(8,128)}, f32[180,8,128]{2,1,0:T(8,128)S(1)}, u32[]{:S(2)}) copy-start(f32[180,8,128]{2,1,0:T(8,128)S(1)} %get-tuple-element.37) | copy-start | bytes 2211844
  52.9 3.1 %copy-start.12 = (f32[5,4,180,32]{2,3,1,0:T(8,128)S(1)}, f32[5,4,180,32]{2,3,1,0:T(8,128)}, u32[]{:S(2)}) copy-start(f32[5,4,180,32]{2,3,1,0:T(8,128)} %copy-done.11) | copy-start | bytes 1382404
  52.9 3.1 %copy-start.14 = (f32[5,4,180,32]{2,3,1,0:T(8,128)S(1)}, f32[5,4,180,32]{2,3,1,0:T(8,128)}, u32[]{:S(2)}) copy-start(f32[5,4,180,32]{2,3,1,0:T(8,128)} %copy-done.13) | copy-start | bytes 1382404
  56.0 6.2 %copy-start.20 = (f32[4,2,1024]{2,1,0:T(2,128)S(1)}, f32[4,2,1024]{2,1,0:T(2,128)}, u32[]{:S(2)}) copy-start(f32[4,2,1024]{2,1,0:T(2,128)} %copy.78) | copy-start | bytes 98308
  57.9 139.6 %collective-permute-start.7 = (f32[5,180,8,128]{3,2,1,0:T(8,128)}, f32[5,180,8,128]{3,2,1,0:T(8,128)}, u32[]{:S(2)}, u32[]{:S(2)}) collective-permute-start(f32[5,180,8,128]{3,2,1,0:T(8,128)} %get-tuple-element.40), channel_id=1, source_target_pairs={{0,1},{1,0},{2,3},{3,2},{4,5},{5,4},{6,7},{7,6},{8,9},{9,8},{10,11... | collective-permute-start | bytes 11059208 | tf_op jit(solution)/shard_map/ppermute | solution.py:413
  63.6 115.2 %collective-permute-start.6 = (f32[24,1024]{1,0:T(8,128)}, f32[24,1024]{1,0:T(8,128)}, u32[]{:S(2)}, u32[]{:S(2)}) collective-permute-start(f32[24,1024]{1,0:T(8,128)} %bitcast.129), channel_id=1, source_target_pairs={{2,0},{4,2},{6,4},{8,6},{10,8},{12,10},{14,12},{16,14},{18,16},{20... | collective-permute-start | bytes 294920 | tf_op jit(solution)/shard_map/ppermute | solution.py:428
  65.4 113.4 %collective-permute-start.5 = (f32[24,1024]{1,0:T(8,128)}, f32[24,1024]{1,0:T(8,128)}, u32[]{:S(2)}, u32[]{:S(2)}) collective-permute-start(f32[24,1024]{1,0:T(8,128)} %bitcast.128), channel_id=1, source_target_pairs={{0,2},{2,4},{4,6},{6,8},{8,10},{10,12},{12,14},{14,16},{16,18},{18... | collective-permute-start | bytes 294920 | tf_op jit(solution)/shard_map/ppermute | solution.py:428
  77.3 1.3 copy-start.4
  174.1 3.4 %copy-start.10 = (f32[180,8,128]{2,1,0:T(8,128)S(1)}, f32[180,8,128]{2,1,0:T(8,128)}, u32[]{:S(2)}) copy-start(f32[180,8,128]{2,1,0:T(8,128)} %copy-done.9) | copy-start | bytes 2211844
  174.1 23.4 %copy-start.2 = (f32[4,180,1024]{2,0,1:T(4,128)S(1)}, f32[4,180,1024]{2,0,1:T(4,128)}, u32[]{:S(2)}) copy-start(f32[4,180,1024]{2,0,1:T(4,128)} %param.10) | copy-start | bytes 8847364
  174.1 23.4 %copy-start.3 = (f32[4,180,1024]{2,0,1:T(4,128)S(1)}, f32[4,180,1024]{2,0,1:T(4,128)}, u32[]{:S(2)}) copy-start(f32[4,180,1024]{2,0,1:T(4,128)} %param.11) | copy-start | bytes 8847364
  177.5 20.0 %collective-permute-start.4 = (f32[180,8,128]{2,1,0:T(8,128)S(1)}, f32[180,8,128]{2,1,0:T(8,128)S(1)}, u32[]{:S(2)}, u32[]{:S(2)}) collective-permute-start(f32[180,8,128]{2,1,0:T(8,128)S(1)} %copy-done.10), channel_id=1, source_target_pairs={{1,0},{3,2},{5,4},{7,6},{9,8},{11,10},{13,12},{15,14},{17,16},{19,... | collective-permute-start | bytes 2211848 | tf_op jit(solution)/shard_map/ppermute | solution.py:381
  (6 other events, 5.7 us)

commit v3 on v2

--- a/solution.py
+++ b/solution.py
@@ -3,6 +3,7 @@
 
 import jax
 import jax.numpy as jnp
+import numpy as np
 from jax import lax
 from jax.experimental import pallas as pl
 from jax.experimental.pallas import tpu as pltpu
@@ -18,9 +19,8 @@
 
 
 def angles(left, right, period):
-    turn = (left * right) % period
-    phase = turn.astype(jnp.float32) * (2.0 * math.pi / period)
-    return jnp.cos(phase), jnp.sin(phase)
+    phase = (left * right) % period * (2.0 * math.pi / period)
+    return np.cos(phase).astype(np.float32), np.sin(phase).astype(np.float32)
 
 
 def filter_kernel(
@@ -113,16 +113,13 @@
     nlon = peers * lon_dev
     rows = cutoff.shape[0] // peers
     kpad = (KMAX + 1 + 127) // 128 * 128
-    wave = jnp.arange(kpad, dtype=jnp.int32)
-    place = jnp.arange(lon_dev, dtype=jnp.int32)
-    fwd = jnp.concatenate(angles(place[:, None], wave[None, :], nlon), axis=1)
-    wide = jnp.arange(-1, lon_dev + 1, dtype=jnp.int32)
-    inv = jnp.stack(angles(wave[:, None], wide[None, :] % nlon, nlon))
-    seat = jnp.arange(peers, dtype=jnp.int32) * lon_dev
-    ct, st = angles(seat[:, None, None], wave[None, None, :], nlon)
+    wave = np.arange(kpad)
+    fwd = np.concatenate(angles(np.arange(lon_dev)[:, None], wave[None, :], nlon), axis=1)
+    inv = np.stack(angles(wave[:, None], np.arange(-1, lon_dev + 1)[None, :] % nlon, nlon))
+    ct, st = angles(np.arange(peers)[:, None, None] * lon_dev, wave[None, None, :], nlon)
     mine = lax.dynamic_slice_in_dim(cutoff, lax.axis_index("lon") * rows, rows)
-    weight = jnp.where(wave == 0, 1.0 / nlon, 2.0 / nlon)
-    mask = jnp.where(wave[None, :] <= mine[:, None], weight[None, :], 0.0)
+    weight = np.where(wave == 0, 1.0 / nlon, 2.0 / nlon).astype(np.float32)
+    mask = jnp.where(jnp.asarray(wave, jnp.int32)[None, :] <= mine[:, None], weight[None, :], 0.0)
     mask = jnp.tile(mask, (cols // rows, 1))
     vmem = pl.BlockSpec(memory_space=pltpu.VMEM)
     dma = pltpu.SemaphoreType.DMA
@@ -169,7 +166,7 @@
     tiles = rows // levels
     flat_c = cot.reshape(fields * chunk * rows, 128)
     flat_v = vw.reshape(chunk * rows, 128)
-    *sends, tail = outs
+    sends = outs[: 1 if choose else 2]
 
     def level(ref, count, k):
         return ref[pl.ds(k, count * tiles, stride=levels), :] if levels > 1 else ref[...]
@@ -177,19 +174,21 @@
     def product(k, sign, out):
         c = level(flat_c, fields * chunk, k).reshape(fields, chunk, tiles, 128)
         v = level(flat_v, chunk, k).reshape(1, chunk, tiles, 128)
-        out[...] = sign * (v * c)
-
+        out[:fields] = sign * (v * c)
+
+    flat_t = cot.at[2].reshape(chunk * rows, 128)
+    total = level(flat_t, chunk, 0)
+    for k in range(1, levels):
+        total = total + level(flat_t, chunk, k)
+    total = total.reshape(chunk, tiles, 128)
     if choose:
+        sends[0][fields] = jnp.where(seat[0] == 0, 0.0, total)
         pl.when(seat[0] == 0)(lambda: product(levels - 1, -1.0, sends[0]))
         pl.when(seat[0] != 0)(lambda: product(0, 1.0, sends[0]))
     else:
         product(0, 1.0, sends[0])
         product(levels - 1, -1.0, sends[1])
-    flat_t = cot.at[2].reshape(chunk * rows, 128)
-    total = level(flat_t, chunk, 0)
-    for k in range(1, levels):
-        total = total + level(flat_t, chunk, k)
-    tail[...] = total.reshape(chunk, tiles, 128)
+        outs[2][...] = total
 
 
 def edges_of(seat, cot, vw, levels, choose):
@@ -197,10 +196,11 @@
     tiles = rows // levels
     chunk = chunk_of(lon)
     n = 1 if choose else 2
+    wide = fields + 1 if choose else fields
     return pl.pallas_call(
         functools.partial(edge_kernel, levels, choose),
-        out_shape=[jax.ShapeDtypeStruct((fields, lon, tiles, 128), jnp.float32)] * n
-        + [jax.ShapeDtypeStruct((lon, tiles, 128), jnp.float32)],
+        out_shape=[jax.ShapeDtypeStruct((wide, lon, tiles, 128), jnp.float32)] * n
+        + [jax.ShapeDtypeStruct((lon, tiles, 128), jnp.float32)] * (n - 1),
         grid_spec=pltpu.PrefetchScalarGridSpec(
             num_scalar_prefetch=1,
             grid=(lon // chunk,),
@@ -208,8 +208,8 @@
                 pl.BlockSpec((fields, chunk, rows, 128), lambda g, s: (0, g, 0, 0)),
                 pl.BlockSpec((chunk, rows, 128), lambda g, s: (g, 0, 0)),
             ],
-            out_specs=[pl.BlockSpec((fields, chunk, tiles, 128), lambda g, s: (0, g, 0, 0))] * n
-            + [pl.BlockSpec((chunk, tiles, 128), lambda g, s: (g, 0, 0))],
+            out_specs=[pl.BlockSpec((wide, chunk, tiles, 128), lambda g, s: (0, g, 0, 0))] * n
+            + [pl.BlockSpec((chunk, tiles, 128), lambda g, s: (g, 0, 0))] * (n - 1),
         ),
         compiler_params=pltpu.CompilerParams(vmem_limit_bytes=24 << 20),
         cost_estimate=pl.CostEstimate(flops=10_000_000, bytes_accessed=22_000_000, transcendentals=0),
@@ -224,8 +224,11 @@
     return flux
 
 
-def stencil_kernel(levels, steps, n_edge, seat, cot, vw, zc, mc, tail, smooth, halo, *rest):
+def stencil_kernel(levels, steps, n_edge, seat, cot, vw, zc, mc, smooth, halo, *rest):
     edges = rest[:n_edge]
+    tail = edges[0].at[5] if n_edge == 1 else rest[n_edge]
+    rest = rest[1:] if n_edge > 1 else rest
+    edge_at = (1 - seat[0]) * (levels - 1)
     out, ready, final, wait, prior, spread, below_ref, sems, last_sem = rest[n_edge:]
     _, chunk, rows, _ = cot.shape
     tiles = rows // levels
@@ -269,8 +272,7 @@
     def one(l, _):
         for f in range(5):
             if n_edge == 1:
-                pl.when(seat[0] == 0)(lambda: put(spread.at[0, f], levels - 1, edges[0][f, l]))
-                pl.when(seat[0] != 0)(lambda: put(spread.at[0, f], 0, edges[0][f, l]))
+                put(spread.at[0, f], edge_at, edges[0][f, l])
             else:
                 put(spread.at[0, f], levels - 1, edges[0][f, l])
                 put(spread.at[1, f], 0, edges[1][f, l])
@@ -327,7 +329,7 @@
         end.wait()
 
 
-def stencil(seat, cot, vw, zc, mc, tail, smooth, halo, edges, levels):
+def stencil(seat, cot, vw, zc, mc, smooth, halo, edges, levels):
     _, lon, rows, _ = cot.shape
     tiles = rows // levels
     chunk = chunk_of(lon)
@@ -335,21 +337,25 @@
     field = lambda n: pl.BlockSpec((5, chunk, n, 128), lambda g, s: (0, g, 0, 0))
     plain = lambda n: pl.BlockSpec((chunk, n, 128), lambda g, s: (g, 0, 0))
     return pl.pallas_call(
-        functools.partial(stencil_kernel, levels, steps, len(edges)),
+        functools.partial(stencil_kernel, levels, steps, min(len(edges), 2)),
         out_shape=jax.ShapeDtypeStruct(cot.shape, jnp.float32),
         grid_spec=pltpu.PrefetchScalarGridSpec(
             num_scalar_prefetch=1,
             grid=(steps,),
-            in_specs=[field(rows), plain(rows), plain(rows), plain(rows), plain(tiles), field(2 * levels),
+            in_specs=[field(rows), plain(rows), plain(rows), plain(rows), field(2 * levels),
                       pl.BlockSpec((5, 2, rows, 128), lambda g, s: (0, 0, 0, 0))]
-            + [field(tiles)] * len(edges),
+            + [pl.BlockSpec((6, chunk, tiles, 128), lambda g, s: (0, g, 0, 0))]
+            if len(edges) == 1
+            else [field(rows), plain(rows), plain(rows), plain(rows), field(2 * levels),
+                  pl.BlockSpec((5, 2, rows, 128), lambda g, s: (0, 0, 0, 0)),
+                  field(tiles), field(tiles), plain(tiles)],
             out_specs=pl.BlockSpec(memory_space=pl.ANY),
             scratch_shapes=[
                 pltpu.VMEM((2, 5, chunk, rows, 128), jnp.float32),
                 pltpu.VMEM((5, 1, rows, 128), jnp.float32),
                 pltpu.VMEM((5, rows, 128), jnp.float32),
                 pltpu.VMEM((5, rows, 128), jnp.float32),
-                pltpu.VMEM((len(edges), 5, rows, 128), jnp.float32),
+                pltpu.VMEM((min(len(edges), 2), 5, rows, 128), jnp.float32),
                 pltpu.VMEM((rows, 128), jnp.float32),
                 pltpu.SemaphoreType.DMA((2,)),
                 pltpu.SemaphoreType.DMA(()),
@@ -360,18 +366,20 @@
             flops=30 * 5 * lon * rows * 128, bytes_accessed=4 * 14 * lon * rows * 128, transcendentals=0
         ),
         name="stencil",
-    )(seat, cot, vw, zc, mc, tail, smooth, halo, *edges)
-
-
-def swap_levels(first, last):
+    )(seat, cot, vw, zc, mc, smooth, halo, *edges)
+
+
+def swap_levels(first, last, total):
     count = lax.axis_size("lev")
     if count == 2:
         seat = lax.axis_index("lev")
-        got = lax.ppermute(jnp.where(seat == 0, last, first), "lev", [(0, 1), (1, 0)])
-        return jnp.where(seat == 0, got, 0.0), jnp.where(seat == 1, got, 0.0)
+        lead = jnp.concatenate([first, total[None]], 0)
+        trail = jnp.concatenate([last, jnp.zeros_like(total)[None]], 0)
+        got = lax.ppermute(jnp.where(seat == 0, trail, lead), "lev", [(0, 1), (1, 0)])
+        return jnp.where(seat == 0, got[:5], 0.0), jnp.where(seat == 1, got[:5], 0.0), got[5]
     up = lax.ppermute(first, "lev", [(i + 1, i) for i in range(count - 1)])
     down = lax.ppermute(last, "lev", [(i, i + 1) for i in range(count - 1)])
-    return up, down
+    return up, down, later_sum(total)
 
 
 def later_sum(local):
@@ -382,13 +390,21 @@
     return total
 
 
-def adjoint_part(cot, vw):
+def ask_levels(cot, vw):
+    return swap_levels(vw[0] * cot[:, 0], vw[-1] * cot[:, -1], cot[2].sum(0))
+
+
+def adjoint_part(cot, vw, up, down, later):
     weighted = vw[None] * cot
-    up, down = swap_levels(weighted[:, 0], weighted[:, -1])
     above = jnp.concatenate([weighted[:, 1:], up[:, None]], 1)
     under = jnp.concatenate([down[:, None], weighted[:, :-1]], 1)
-    below = jnp.flip(jnp.cumsum(jnp.flip(cot[2], 0), 0), 0) + later_sum(cot[2].sum(0))[None]
-    return (cot + (above - under)).at[3].add(-COUPLE_B * below)
+    below = [later + cot[2, -1]]
+    for k in range(cot.shape[1] - 2, -1, -1):
+        below.insert(0, below[0] + cot[2, k])
+    parts = cot + (above - under)
+    return jnp.concatenate(
+        [parts[:3], parts[3:4] - COUPLE_B * jnp.stack(below)[None], parts[4:]], 0
+    )
 
 
 def polar_cut(x):
@@ -401,22 +417,24 @@
     count = lax.axis_size("lev")
     seat = lax.axis_index("lev").astype(jnp.int32)[None]
     cot, vw = to_rows(cotangent), to_rows(vertical_wind)
-    *sends, local = edges_of(seat, cot, vw, levels, count == 2)
-
     polar_cot = jnp.swapaxes(polar_cut(cotangent), 2, 3)
     polar_vw = jnp.swapaxes(polar_cut(vertical_wind), 1, 2)
-    polar = adjoint_part(polar_cot, polar_vw)
-    ends_adj = adjoint_part(cotangent[:, :, :: lon_dev - 1], vertical_wind[:, :: lon_dev - 1])
-
-    polar, ends_adj, local, *sends = lax.optimization_barrier((polar, ends_adj, local, *sends))
+    polar_got = ask_levels(polar_cot, polar_vw)
+    ends_cot, ends_vw = cotangent[:, :, :: lon_dev - 1], vertical_wind[:, :: lon_dev - 1]
+    ends_got = ask_levels(ends_cot, ends_vw)
+
+    sends = edges_of(seat, cot, vw, levels, count == 2)
+    polar_got, ends_got, sends = lax.optimization_barrier((polar_got, ends_got, sends))
     if count == 2:
         edges = [lax.ppermute(sends[0], "lev", [(0, 1), (1, 0)])]
     else:
         edges = [
             lax.ppermute(sends[0], "lev", [(i + 1, i) for i in range(count - 1)]),
             lax.ppermute(sends[1], "lev", [(i, i + 1) for i in range(count - 1)]),
+            later_sum(sends[2]),
         ]
-    tail = later_sum(local)
+    polar = adjoint_part(polar_cot, polar_vw, *polar_got)
+    ends_adj = adjoint_part(ends_cot, ends_vw, *ends_got)
 
     rows = 2 * POLAR // peers
     grouped = polar.reshape(5 * levels, peers, rows, lon_dev)
@@ -441,7 +459,7 @@
     halo_f = jnp.concatenate([outer[0], halo_adj[..., POLAR : lat - POLAR], outer[1]], 3)
     halo = jnp.stack(coupled(halo_zc, [halo_f[f] for f in range(5)], 0))
     out = stencil(
-        seat, cot, vw, to_rows(zonal_coef), to_rows(merid_coef), tail, smooth, to_rows(halo), edges, levels
+        seat, cot, vw, to_rows(zonal_coef), to_rows(merid_coef), smooth, to_rows(halo), edges, levels
     )
     return from_rows(out, levels)
 

time: 241 us -> 195 us (0.81)
  waiting for transfers between devices: 16.2 us -> 0.01 us
  starting transfers between devices: 13.7 us -> 3.94 us
  Pallas kernels: 125 us -> 116 us
  other arithmetic: 24.4 us -> 17.5 us
  local copies, waits for them, and re-layouts: 59.4 us -> 55.9 us
    ppermute x5 -> x2, waiting for transfers between devices: 16.2 us -> 0.01 us  [swap_levels(): lax.ppermute(jnp.where(seat == 0, trail, lead), 'lev', [(0, 1), (1, 0)])]
    pallas_call x1, Pallas kernels: 41.9 us -> 29.2 us  [stencil(): pl.pallas_call(functools.partial(stencil_kernel, levels, steps, min(len(e...]
    rev x3 -> x0, local copies, waits for them, and re-layouts: 5.29 us -> none  [the longest x1 2.81 us: adjoint_part(): jnp.flip(jnp.cumsum(jnp.flip(cot[2], 0), 0), 0)]
    ppermute x5 -> x2, starting transfers between devices: 6.51 us -> 1.47 us  [swap_levels(): lax.ppermute(jnp.where(seat == 0, trail, lead), 'lev', [(0, 1), (1, 0)])]
    pallas_call x1, Pallas kernels: 78.6 us -> 81.9 us  [polar_filter(): pl.pallas_call(functools.partial(filter_kernel, peers), out_shape=jax.Sha...]
    sin x2 -> x0, other arithmetic: 3.29 us -> none  [angles(): return (jnp.cos(phase), jnp.sin(phase))]
    select_n x5, other arithmetic: 0.91 us -> 3.65 us  [the longest x2 1.92 us: swap_levels(): jnp.where(seat == 1, got[:5], 0.0)]
    unnamed x53 -> x59, local copies, waits for them, and re-layouts: 24.3 us -> 26.7 us
  transfers between devices with their start and end apart: 8 -> 5, of which waited for: 1 -> 0; matrix products, arithmetic and copies ran while one was open for 29% -> 25% of each run, Pallas kernels for 35% -> 45%
where the time goes in v3:
time: 195 us; the launch traced here: 194 us
  Pallas kernels  116 us (59%)
  local copies, waits for them, and re-layouts  55.9 us (29%)
  other arithmetic  17.5 us (9%)
  starting transfers between devices  3.94 us (2%)
    pallas_call x1, Pallas kernels, polar_filter(): pl.pallas_call(functools.partial(filter_kernel, peers), out_shape=jax.Sha...  81.9 us
    pallas_call x1, Pallas kernels, stencil(): pl.pallas_call(functools.partial(stencil_kernel, levels, steps, min(len(e...  29.2 us
    unnamed x59, local copies, waits for them, and re-layouts  26.7 us
    slice x2, local copies, waits for them, and re-layouts, polar_cut(): return jnp.concatenate([x[..., :POLAR], x[..., x.shape[-1] - POLAR:]], -1)  5.73 us
    concatenate x1, other arithmetic, body(): jnp.concatenate([jnp.pad(north, (*gap, (0, 128 - POLAR))), jnp.pad(south,...  5.08 us
    pallas_call x1, Pallas kernels, edges_of(): pl.pallas_call(functools.partial(edge_kernel, levels, choose), out_shape=...  4.92 us
    reshape x2, local copies, waits for them, and re-layouts, body(): smoothed = smoothed.reshape(2, peers // 2, 5, levels, rows, lon_dev + 2)  4.38 us
  transfers between devices with their start and end apart: 5, of which 0 were waited for; matrix products, arithmetic and copies ran while one was open for 25% of the time, Pallas kernels for 45%

profile of v3, /device:TPU:27, one launch (start us, length us, event | category | flops | bytes accessed | tf_op | source)
XLA Modules:
  0.0 194.1 jit_solution(4437713573748713603)
XLA Ops:
  4.0 1.2 collective-permute-start.1
  5.2 1.4 fusion.31
  6.6 4.4 %fusion.30 = (f32[5,4,180,32]{3,1,2,0:T(4,128)}, f32[5,4,180,32]{3,1,2,0:T(4,128)S(1)}) fusion(f32[5,4,180,1024]{3,1,2,0:T(4,128)} %param.11), kind=kLoop, calls=%fused_computation.91 | loop fusion | bytes 1843200 | tf_op jit(solution)/shard_map/slice | solution.py:411
  11.4 2.3 %copy.70 = f32[5,4,180,32]{2,3,1,0:T(8,128)S(1)} copy(f32[5,4,180,32]{3,1,2,0:T(4,128)} %get-tuple-element.25) | data formatting | bytes 921600
  13.7 1.8 copy.71
  18.5 3.2 %fusion.33 = (f32[5,3,64,180]{3,2,1,0:T(8,128)}, f32[5,3,64,180]{3,2,1,0:T(8,128)}) fusion(f32[5,4,64,180]{3,2,1,0:T(8,128)} %broadcast_multiply_fusion), kind=kLoop, calls=%fused_computation.94 | loop fusion | bytes 2764800 | tf_op jit(solution)/shard_map/slice | solution.py:400
  22.7 5.2 %copy-done = f32[5,4,180,1024]{3,1,2,0:T(4,128)S(1)} copy-done((f32[5,4,180,1024]{3,1,2,0:T(4,128)S(1)}, f32[5,4,180,1024]{3,1,2,0:T(4,128)}, u32[]{:S(2)}) %copy-start) | copy-done | bytes 14745624
  27.8 4.9 %edges.1 = f32[6,180,8,128]{3,2,1,0:T(8,128)} custom-call(s32[1]{0:T(128)} %bitcast.seat, f32[5,180,32,128]{3,2,1,0:T(8,128)S(1)} %bitcast.193, f32[180,32,128]{2,1,0:T(8,128)S(1)} %bitcast.194), custom_call_target="tpu_custom_call" | custom-call | flops 10000000 | bytes 22000000 | tf_op jit(solution)/shard_map/edges/pallas_call | solution.py:200
  40.3 1.2 collective-permute-start.4
  45.1 2.6 %reshape.237 = f32[20,16,4,180]{3,2,1,0:T(4,128)} reshape(f32[5,4,64,180]{3,2,1,0:T(8,128)} %pad_maximum_fusion) | data formatting | bytes 1843200 | tf_op jit(solution)/shard_map/reshape | solution.py:440
  47.7 2.7 %copy.52 = f32[16,20,4,180]{3,2,1,0:T(4,128)} copy(f32[16,20,4,180]{3,2,0,1:T(4,128)} %bitcast.204) | data formatting | bytes 1843200 | tf_op jit(solution)/shard_map/transpose | solution.py:441
  50.4 2.7 %reshape.238.x_ref = f32[16,80,180]{2,1,0:T(8,128)} reshape(f32[16,20,4,180]{3,2,1,0:T(4,128)} %copy.52) | data formatting | bytes 1843200 | tf_op jit(solution)/shard_map/reshape | solution.py:441
  53.1 1.3 copy-done.5
  56.6 81.9 %polar_filter.1 = f32[16,80,182]{2,1,0:T(8,128)S(1)} custom-call(f32[16,80,180]{2,1,0:T(8,128)S(1)} %copy-done.5, f32[180,768]{1,0:T(8,128)S(1)} %copy-done.8, f32[2,384,182]{2,1,0:T(8,128)S(1)} %copy-done.7, f32[16,1,384]{2,1,0:T(1,128)S(1)} %copy-done.10, f32[16,1,384]{2,1,0:T(1,128)S(1)} %copy-done.9, f32[80,384]{1,0:T(8,128)S(1)} %tile.10.mask_ref), custom_call_target="tpu_custom_call" | custom-call | flops 8000000000 | bytes 60000000 | tf_op jit(solution)/shard_map/polar_filter/pallas_call | solution.py:126
  139.7 2.6 %reshape.239 = f32[2,8,5,4,4,182]{5,4,3,2,1,0:T(4,128)} reshape(f32[16,80,182]{2,1,0:T(8,128)} %copy-done.6) | data formatting | bytes 1863680 | tf_op jit(solution)/shard_map/reshape | solution.py:451
  142.3 1.8 copy.53
  144.1 1.3 fusion.32
  145.4 2.9 %copy.77 = f32[5,182,1,4,32]{4,3,1,0,2:T(4,128)} copy(f32[5,182,1,4,32]{1,3,4,2,0:T(4,128)} %get-tuple-element.30) | data formatting | bytes 931840
  148.3 2.9 %copy.78 = f32[5,182,1,4,32]{4,3,1,0,2:T(4,128)} copy(f32[5,182,1,4,32]{1,3,4,2,0:T(4,128)} %get-tuple-element.31) | data formatting | bytes 931840
  152.6 5.1 %fusion.smooth = f32[5,180,8,128]{3,2,1,0:T(8,128)} fusion(f32[5,182,4,32]{3,2,1,0:T(4,128)} %bitcast.202, f32[5,182,4,32]{3,2,1,0:T(4,128)} %bitcast.200), kind=kLoop, calls=%fused_computation.1 | loop fusion | flops 4608000 | bytes 4618240 | tf_op jit(solution)/shard_map/concatenate | solution.py:455
  159.0 2.0 %copy-done.2 = f32[5,180,8,128]{3,2,1,0:T(8,128)S(1)} copy-done((f32[5,180,8,128]{3,2,1,0:T(8,128)S(1)}, f32[5,180,8,128]{3,2,1,0:T(8,128)}, u32[]{:S(2)}) %copy-start.2) | copy-done | bytes 3686424
  161.1 1.8 copy-done.3
  162.9 1.8 copy-done.4
  164.7 29.2 %stencil.1 = f32[5,180,32,128]{3,2,1,0:T(8,128)} custom-call(s32[1]{0:T(128)} %bitcast.seat, f32[5,180,32,128]{3,2,1,0:T(8,128)} %bitcast.192, f32[180,32,128]{2,1,0:T(8,128)S(1)} %bitcast.195, f32[180,32,128]{2,1,0:T(8,128)S(1)} %bitcast.196, f32[180,32,128]{2,1,0:T(8,128)S(1)} %bitcast.197, f32[5,180,8,128]{3,2,1,0:T(8,128)S(1)} %copy-done.2, ...), custom_call_target="tpu_custom_call" | custom-call | flops 110592000 | bytes 41287680 | tf_op jit(solution)/shard_map/stencil/pallas_call | solution.py:339
  (114 shorter events, 25.1 us)
Async XLA Ops:
  4.0 28.8 %collective-permute-start.1 = (f32[6,2,1024]{2,1,0:T(2,128)}, f32[6,2,1024]{2,1,0:T(2,128)}, u32[]{:S(2)}, u32[]{:S(2)}) collective-permute-start(f32[6,2,1024]{2,1,0:T(2,128)} %maximum_select_fusion.1), channel_id=1, source_target_pairs={{0,1},{1,0},{2,3},{3,2},{4,5},{5,4},{6,7},{7,6},{8,9},{9,8},{10,11... | collective-permute-start | bytes 147464 | tf_op jit(solution)/shard_map/ppermute | solution.py:378
  13.7 3.5 %copy-start.11 = (f32[5,4,180,32]{2,3,1,0:T(8,128)}, f32[5,4,180,32]{2,3,1,0:T(8,128)S(1)}, u32[]{:S(2)}) copy-start(f32[5,4,180,32]{2,3,1,0:T(8,128)S(1)} %copy.70) | copy-start | bytes 1382404
  15.6 1.6 copy-start.13
  15.7 1.3 copy-start.15
  17.0 17.3 %collective-permute-start = (f32[6,64,180]{2,1,0:T(8,128)}, f32[6,64,180]{2,1,0:T(8,128)}, u32[]{:S(2)}, u32[]{:S(2)}) collective-permute-start(f32[6,64,180]{2,1,0:T(8,128)} %maximum_select_fusion), channel_id=1, source_target_pairs={{0,1},{1,0},{2,3},{3,2},{4,5},{5,4},{6,7},{7,6},{8,9},{9,8},{10,11... | collective-permute-start | bytes 829448 | tf_op jit(solution)/shard_map/ppermute | solution.py:378
  17.2 1.2 copy-start.20
  18.5 3.2 %copy-start.23 = (s32[64]{0:T(128)S(1)}, s32[64]{0:T(128)}, u32[]{:S(2)}) copy-start(s32[64]{0:T(128)} %param.15) | copy-start | bytes 772
  18.5 3.3 %copy-start.22 = (f32[384]{0:T(512)S(1)}, f32[384]{0:T(512)}, u32[]{:S(2)}) copy-start(f32[384]{0:T(512)} %constant.55) | copy-start | bytes 4612
  18.5 4.2 %copy-start.1 = (f32[4,180,1024]{2,0,1:T(4,128)S(1)}, f32[4,180,1024]{2,0,1:T(4,128)}, u32[]{:S(2)}) copy-start(f32[4,180,1024]{2,0,1:T(4,128)} %param.14) | copy-start | bytes 8847364
  22.6 5.2 %copy-start = (f32[5,4,180,1024]{3,1,2,0:T(4,128)S(1)}, f32[5,4,180,1024]{3,1,2,0:T(4,128)}, u32[]{:S(2)}) copy-start(f32[5,4,180,1024]{3,1,2,0:T(4,128)} %param.11) | copy-start | bytes 44236804
  32.8 5.2 %copy-start.19 = (f32[5,4,2,1024]{3,1,2,0:T(4,128)S(1)}, f32[5,4,2,1024]{3,1,2,0:T(4,128)}, u32[]{:S(2)}) copy-start(f32[5,4,2,1024]{3,1,2,0:T(4,128)} %copy-done.18) | copy-start | bytes 491524
  34.3 7.2 %copy-start.17 = (f32[5,3,64,180]{3,2,1,0:T(8,128)S(1)}, f32[5,3,64,180]{3,2,1,0:T(8,128)}, u32[]{:S(2)}) copy-start(f32[5,3,64,180]{3,2,1,0:T(8,128)} %get-tuple-element.35) | copy-start | bytes 2073604
  35.3 6.3 %copy-start.16 = (f32[5,3,64,180]{3,2,1,0:T(8,128)S(1)}, f32[5,3,64,180]{3,2,1,0:T(8,128)}, u32[]{:S(2)}) copy-start(f32[5,3,64,180]{3,2,1,0:T(8,128)} %get-tuple-element.34) | copy-start | bytes 2073604
  36.4 5.2 %copy-start.12 = (f32[5,4,180,32]{2,3,1,0:T(8,128)S(1)}, f32[5,4,180,32]{2,3,1,0:T(8,128)}, u32[]{:S(2)}) copy-start(f32[5,4,180,32]{2,3,1,0:T(8,128)} %copy-done.11) | copy-start | bytes 1382404
  36.4 5.2 %copy-start.14 = (f32[5,4,180,32]{2,3,1,0:T(8,128)S(1)}, f32[5,4,180,32]{2,3,1,0:T(8,128)}, u32[]{:S(2)}) copy-start(f32[5,4,180,32]{2,3,1,0:T(8,128)} %copy-done.13) | copy-start | bytes 1382404
  39.1 118.6 %collective-permute-start.2 = (f32[24,1024]{1,0:T(8,128)}, f32[24,1024]{1,0:T(8,128)S(1)}, u32[]{:S(2)}, u32[]{:S(2)}) collective-permute-start(f32[24,1024]{1,0:T(8,128)} %get-tuple-element.42), channel_id=1, source_target_pairs={{0,2},{2,4},{4,6},{6,8},{8,10},{10,12},{12,14},{14,16},{16,18},{18... | collective-permute-start | bytes 294920 | tf_op jit(solution)/shard_map/ppermute | solution.py:446
  39.6 118.2 %collective-permute-start.3 = (f32[24,1024]{1,0:T(8,128)S(1)}, f32[24,1024]{1,0:T(8,128)S(1)}, u32[]{:S(2)}, u32[]{:S(2)}) collective-permute-start(f32[24,1024]{1,0:T(8,128)S(1)} %get-tuple-element.43), channel_id=1, source_target_pairs={{2,0},{4,2},{6,4},{8,6},{10,8},{12,10},{14,12},{16,14},{18,16},{20... | collective-permute-start | bytes 294920 | tf_op jit(solution)/shard_map/ppermute | solution.py:446
  40.3 118.7 %collective-permute-start.4 = (f32[6,180,8,128]{3,2,1,0:T(8,128)}, f32[6,180,8,128]{3,2,1,0:T(8,128)}, u32[]{:S(2)}, u32[]{:S(2)}) collective-permute-start(f32[6,180,8,128]{3,2,1,0:T(8,128)} %edges.1), channel_id=1, source_target_pairs={{0,1},{1,0},{2,3},{3,2},{4,5},{5,4},{6,7},{7,6},{8,9},{9,8},{10,11... | collective-permute-start | bytes 13271048 | tf_op jit(solution)/shard_map/ppermute | solution.py:429
  50.4 2.7 %copy-start.9 = (f32[16,1,384]{2,1,0:T(1,128)S(1)}, f32[16,1,384]{2,1,0:T(1,128)}, u32[]{:S(2)}) copy-start(f32[16,1,384]{2,1,0:T(1,128)} %constant.42.clone.st_ref) | copy-start | bytes 73732
  50.4 2.7 %copy-start.10 = (f32[16,1,384]{2,1,0:T(1,128)S(1)}, f32[16,1,384]{2,1,0:T(1,128)}, u32[]{:S(2)}) copy-start(f32[16,1,384]{2,1,0:T(1,128)} %constant.41.clone.ct_ref) | copy-start | bytes 73732
  53.1 1.3 copy-start.5
  159.0 2.0 %copy-start.2 = (f32[5,180,8,128]{3,2,1,0:T(8,128)S(1)}, f32[5,180,8,128]{3,2,1,0:T(8,128)}, u32[]{:S(2)}) copy-start(f32[5,180,8,128]{3,2,1,0:T(8,128)} %fusion.smooth) | copy-start | bytes 11059204
  161.1 1.8 copy-start.3
  162.9 1.8 copy-start.4
  (5 other events, 4.7 us)

commit v4 on v3

--- a/solution.py
+++ b/solution.py
@@ -24,7 +24,7 @@
 
 
 def filter_kernel(
-    peers, x_ref, fwd_ref, inv_ref, ct_ref, st_ref, mask_ref, out_ref, held, made,
+    peers, packed, x_ref, fwd_ref, inv_ref, ct_ref, st_ref, mask_ref, out_ref, held, made,
     own_sem, send_a, recv_a, send_b, recv_b,
 ):
     me = lax.axis_index("lon")
@@ -72,34 +72,49 @@
     own = pltpu.make_async_copy(x_ref.at[me], held.at[me], own_sem)
     own.start()
     own.wait()
-    lax.fori_loop(1, peers, lambda o, c: (in_copy(o).wait_recv(), c)[1], 0)
-
-    cols = held.shape[1]
+    cols = mask_ref.shape[0]
+    half = cols // 2
     zero = jnp.zeros((cols, kpad), jnp.float32)
+    dot = functools.partial(jnp.dot, precision=HIGHEST, preferred_element_type=jnp.float32)
 
     def gather(s, carry):
         a, b = carry
-        both = jnp.dot(held[s], fwd_ref[...], precision=HIGHEST, preferred_element_type=jnp.float32)
+        if packed:
+            ends = held[s, cols:]
+            ends = jnp.concatenate([ends[:, :64], ends[:, 64:]], 0)
+            both = dot(held[s, :cols], fwd_ref[:128]) + dot(ends, fwd_ref[128:])
+        else:
+            both = dot(held[s], fwd_ref[...])
         c, v = both[:, :kpad], both[:, kpad:]
         ct, st = ct_ref[s], st_ref[s]
         return a + (ct * c - st * v), b + (st * c + ct * v)
 
-    a, b = lax.fori_loop(0, peers, gather, (zero, zero))
+    def arrive(o, carry):
+        in_copy(o).wait_recv()
+        return gather(lax.rem(me + o, peers), carry)
+
+    a, b = lax.fori_loop(1, peers, arrive, gather(me, (zero, zero)))
     a = a * mask_ref[...]
     b = b * mask_ref[...]
 
-    def spread(d, carry):
-        a, b = carry
+    def spread(d):
         ct, st = ct_ref[d], st_ref[d]
-        made[d] = jnp.dot(
-            a * ct + b * st, inv_ref[0], precision=HIGHEST, preferred_element_type=jnp.float32
-        ) + jnp.dot(
-            b * ct - a * st, inv_ref[1], precision=HIGHEST, preferred_element_type=jnp.float32
-        )
-        return carry
-
-    lax.fori_loop(0, peers, spread, (a, b))
-    lax.fori_loop(1, peers, lambda o, c: (back_copy(o).start(), c)[1], 0)
+        p, q = a * ct + b * st, b * ct - a * st
+        if packed:
+            y = dot(p, inv_ref[0]) + dot(q, inv_ref[1])
+            made[d, :cols] = y[:, :128]
+            made[d, cols:] = jnp.concatenate([y[:half, 128:], y[half:, 128:]], 1)
+        else:
+            made[d] = dot(p, inv_ref[0]) + dot(q, inv_ref[1])
+
+    def depart(o, _):
+        spread(lax.rem(me + o, peers))
+        pl.when(o > 1)(lambda: back_copy(o - 1).start())
+        return 0
+
+    lax.fori_loop(1, peers, depart, 0)
+    spread(me)
+    back_copy(peers - 1).start()
     mine = pltpu.make_async_copy(made.at[me], out_ref.at[me], own_sem)
     mine.start()
     mine.wait()
@@ -116,6 +131,17 @@
     wave = np.arange(kpad)
     fwd = np.concatenate(angles(np.arange(lon_dev)[:, None], wave[None, :], nlon), axis=1)
     inv = np.stack(angles(wave[:, None], np.arange(-1, lon_dev + 1)[None, :] % nlon, nlon))
+    over, wider = lon_dev - 128, lon_dev + 2 - 128
+    packed = over > 0 and wider <= 64 and cols % 16 == 0
+    half = cols // 2
+    if packed:
+        fwd = np.pad(fwd, ((0, 64 - over), (0, 0)))
+        inv = np.pad(inv, ((0, 0), (0, 0), (0, 64 - wider)))
+        ends = jnp.pad(x[..., 128:], ((0, 0), (0, 0), (0, 64 - over)))
+        x = jnp.concatenate([x[..., :128], jnp.concatenate([ends[:, :half], ends[:, half:]], 2)], 1)
+        shape = (peers, cols + half, 128)
+    else:
+        shape = (peers, cols, lon_dev + 2)
     ct, st = angles(np.arange(peers)[:, None, None] * lon_dev, wave[None, None, :], nlon)
     mine = lax.dynamic_slice_in_dim(cutoff, lax.axis_index("lon") * rows, rows)
     weight = np.where(wave == 0, 1.0 / nlon, 2.0 / nlon).astype(np.float32)
@@ -123,14 +149,14 @@
     mask = jnp.tile(mask, (cols // rows, 1))
     vmem = pl.BlockSpec(memory_space=pltpu.VMEM)
     dma = pltpu.SemaphoreType.DMA
-    return pl.pallas_call(
-        functools.partial(filter_kernel, peers),
-        out_shape=jax.ShapeDtypeStruct((peers, cols, lon_dev + 2), jnp.float32),
+    y = pl.pallas_call(
+        functools.partial(filter_kernel, peers, packed),
+        out_shape=jax.ShapeDtypeStruct(shape, jnp.float32),
         in_specs=[vmem] * 6,
         out_specs=vmem,
         scratch_shapes=[
-            pltpu.VMEM((peers, cols, lon_dev), jnp.float32),
-            pltpu.VMEM((peers, cols, lon_dev + 2), jnp.float32),
+            pltpu.VMEM(x.shape, jnp.float32),
+            pltpu.VMEM(shape, jnp.float32),
             dma(()), dma((peers,)), dma((peers,)), dma((peers,)), dma((peers,)),
         ],
         compiler_params=pltpu.CompilerParams(
@@ -139,6 +165,10 @@
         cost_estimate=pl.CostEstimate(flops=8_000_000_000, bytes_accessed=60_000_000, transcendentals=0),
         name="polar_filter",
     )(x, fwd, inv, ct, st, mask)
+    if not packed:
+        return y
+    ends = jnp.concatenate([y[:, cols:, :wider], y[:, cols:, 64 : 64 + wider]], 1)
+    return jnp.concatenate([y[:, :cols], ends], 2)
 
 
 def to_rows(x):

time: 195 us -> 175 us (0.90)
  Pallas kernels: 116 us -> 95.8 us
    pallas_call x1, Pallas kernels: 81.9 us -> 61.4 us  [polar_filter(): pl.pallas_call(functools.partial(filter_kernel, peers, packed), out_shape...]
    unnamed x59 -> x51, local copies, waits for them, and re-layouts: 26.7 us -> 22.8 us
  transfers between devices with their start and end apart: 5 -> 5, of which waited for: 0 -> 0; matrix products, arithmetic and copies ran while one was open for 25% -> 30% of each run, Pallas kernels for 45% -> 38%
where the time goes in v4:
time: 175 us; the launch traced here: 172 us
  Pallas kernels  95.8 us (55%)
  local copies, waits for them, and re-layouts  55.3 us (32%)
  other arithmetic  15.9 us (9%)
  starting transfers between devices  4.58 us (3%)
    pallas_call x1, Pallas kernels, polar_filter(): pl.pallas_call(functools.partial(filter_kernel, peers, packed), out_shape...  61.4 us
    pallas_call x1, Pallas kernels, stencil(): pl.pallas_call(functools.partial(stencil_kernel, levels, steps, min(len(e...  29.5 us
    unnamed x51, local copies, waits for them, and re-layouts  22.8 us
    slice x2, local copies, waits for them, and re-layouts, polar_cut(): return jnp.concatenate([x[..., :POLAR], x[..., x.shape[-1] - POLAR:]], -1)  5.71 us
    concatenate x1, other arithmetic, body(): jnp.concatenate([jnp.pad(north, (*gap, (0, 128 - POLAR))), jnp.pad(south,...  5.08 us
    pallas_call x1, Pallas kernels, edges_of(): pl.pallas_call(functools.partial(edge_kernel, levels, choose), out_shape=...  4.92 us
    reshape x2, local copies, waits for them, and re-layouts, body(): smoothed = smoothed.reshape(2, peers // 2, 5, levels, rows, lon_dev + 2)  4.39 us
    slice x2, local copies, waits for them, and re-layouts, adjoint_part(): under = jnp.concatenate([down[:, None], weighted[:, :-1]], 1)  3.81 us
  transfers between devices with their start and end apart: 5, of which 0 were waited for; matrix products, arithmetic and copies ran while one was open for 30% of the time, Pallas kernels for 38%

profile of v4, /device:TPU:27, one launch (start us, length us, event | category | flops | bytes accessed | tf_op | source)
XLA Modules:
  0.0 172.2 jit_solution(17609712372745457997)
XLA Ops:
  2.7 1.2 collective-permute-start.1
  3.9 1.4 fusion.31
  5.3 4.3 %fusion.30 = (f32[5,4,180,32]{3,1,2,0:T(4,128)S(1)}, f32[5,4,180,32]{3,1,2,0:T(4,128)}) fusion(f32[5,4,180,1024]{3,1,2,0:T(4,128)} %param.11), kind=kLoop, calls=%fused_computation.95 | loop fusion | bytes 1843200 | tf_op jit(solution)/shard_map/slice | solution.py:441
  10.1 1.8 %copy.70 = f32[5,4,180,32]{2,3,1,0:T(8,128)S(1)} copy(f32[5,4,180,32]{3,1,2,0:T(4,128)S(1)} %get-tuple-element.25) | data formatting | bytes 921600
  11.9 2.6 %copy.71 = f32[5,4,180,32]{2,3,1,0:T(8,128)S(1)} copy(f32[5,4,180,32]{3,1,2,0:T(4,128)} %get-tuple-element.26) | data formatting | bytes 921600
  18.0 3.1 %fusion.33 = (f32[5,3,64,180]{3,2,1,0:T(8,128)}, f32[5,3,64,180]{3,2,1,0:T(8,128)}) fusion(f32[5,4,64,180]{3,2,1,0:T(8,128)} %broadcast_multiply_fusion), kind=kLoop, calls=%fused_computation.98 | loop fusion | bytes 2764800 | tf_op jit(solution)/shard_map/slice | solution.py:430
  23.6 5.2 %copy-done = f32[5,4,180,1024]{3,1,2,0:T(4,128)S(1)} copy-done((f32[5,4,180,1024]{3,1,2,0:T(4,128)S(1)}, f32[5,4,180,1024]{3,1,2,0:T(4,128)}, u32[]{:S(2)}) %copy-start) | copy-done | bytes 14745624
  28.8 4.9 %edges.1 = f32[6,180,8,128]{3,2,1,0:T(8,128)} custom-call(s32[1]{0:T(128)} %bitcast.seat, f32[5,180,32,128]{3,2,1,0:T(8,128)S(1)} %bitcast.193, f32[180,32,128]{2,1,0:T(8,128)S(1)} %bitcast.194), custom_call_target="tpu_custom_call" | custom-call | flops 10000000 | bytes 22000000 | tf_op jit(solution)/shard_map/edges/pallas_call | solution.py:230
  39.5 1.3 collective-permute-start.4
  42.4 2.7 %reshape.237 = f32[20,16,4,180]{3,2,1,0:T(4,128)} reshape(f32[5,4,64,180]{3,2,1,0:T(8,128)} %pad_maximum_fusion) | data formatting | bytes 1843200 | tf_op jit(solution)/shard_map/reshape | solution.py:470
  45.0 2.7 %copy.52 = f32[16,20,4,180]{3,2,1,0:T(4,128)} copy(f32[16,20,4,180]{3,2,0,1:T(4,128)} %bitcast.204) | data formatting | bytes 1843200 | tf_op jit(solution)/shard_map/transpose | solution.py:471
  47.8 2.7 %reshape.238 = f32[16,80,180]{2,1,0:T(8,128)} reshape(f32[16,20,4,180]{3,2,1,0:T(4,128)} %copy.52) | data formatting | bytes 1843200 | tf_op jit(solution)/shard_map/reshape | solution.py:471
  51.5 1.4 collective-permute-start.2
  54.7 61.4 %polar_filter.1 = f32[16,120,128]{2,1,0:T(8,128)S(1)} custom-call(f32[16,120,128]{2,1,0:T(8,128)S(1)} %maximum_maximum_fusion.1.x_ref, f32[192,768]{1,0:T(8,128)S(1)} %copy-done.6, f32[2,384,192]{2,1,0:T(8,128)S(1)} %copy-done.5, f32[16,1,384]{2,1,0:T(1,128)S(1)} %copy-done.8, f32[16,1,384]{2,1,0:T(1,128)S(1)} %copy-done.7, f32[80,384]{1,0:T(8,128)S(1)} %tile.10.mask_ref), custom_call_target="tpu_custom_call" | custom-call | flops 8000000000 | bytes 60000000 | tf_op jit(solution)/shard_map/polar_filter/pallas_call | solution.py:152
  117.5 2.6 %reshape.239 = f32[2,8,5,4,4,182]{5,4,3,2,1,0:T(4,128)} reshape(f32[16,80,182]{2,1,0:T(8,128)} %maximum_maximum_fusion) | data formatting | bytes 1863680 | tf_op jit(solution)/shard_map/reshape | solution.py:481
  120.1 1.8 %copy.53 = f32[2,8,5,4,4,182]{5,3,4,1,0,2:T(4,128)S(1)} copy(f32[2,8,5,4,4,182]{5,4,3,2,1,0:T(4,128)} %reshape.239) | data formatting | bytes 1863680 | tf_op jit(solution)/shard_map/reshape | solution.py:481
  121.9 1.3 fusion.32
  123.2 2.9 %copy.77 = f32[5,182,1,4,32]{4,3,1,0,2:T(4,128)} copy(f32[5,182,1,4,32]{1,3,4,2,0:T(4,128)} %get-tuple-element.30) | data formatting | bytes 931840
  126.1 2.9 %copy.78 = f32[5,182,1,4,32]{4,3,1,0,2:T(4,128)} copy(f32[5,182,1,4,32]{1,3,4,2,0:T(4,128)} %get-tuple-element.31) | data formatting | bytes 931840
  130.4 5.1 %fusion.smooth = f32[5,180,8,128]{3,2,1,0:T(8,128)} fusion(f32[5,182,4,32]{3,2,1,0:T(4,128)} %bitcast.202, f32[5,182,4,32]{3,2,1,0:T(4,128)} %bitcast.200), kind=kLoop, calls=%fused_computation.1 | loop fusion | flops 4608000 | bytes 4618240 | tf_op jit(solution)/shard_map/concatenate | solution.py:485
  136.8 2.0 %copy-done.2 = f32[5,180,8,128]{3,2,1,0:T(8,128)S(1)} copy-done((f32[5,180,8,128]{3,2,1,0:T(8,128)S(1)}, f32[5,180,8,128]{3,2,1,0:T(8,128)}, u32[]{:S(2)}) %copy-start.2) | copy-done | bytes 3686424
  138.9 1.8 %copy-done.3 = f32[4,180,1024]{2,0,1:T(4,128)S(1)} copy-done((f32[4,180,1024]{2,0,1:T(4,128)S(1)}, f32[4,180,1024]{2,0,1:T(4,128)}, u32[]{:S(2)}) %copy-start.3) | copy-done | bytes 2949144
  140.7 1.8 %copy-done.4 = f32[4,180,1024]{2,0,1:T(4,128)S(1)} copy-done((f32[4,180,1024]{2,0,1:T(4,128)S(1)}, f32[4,180,1024]{2,0,1:T(4,128)}, u32[]{:S(2)}) %copy-start.4) | copy-done | bytes 2949144
  142.5 29.5 %stencil.1 = f32[5,180,32,128]{3,2,1,0:T(8,128)} custom-call(s32[1]{0:T(128)} %bitcast.seat, f32[5,180,32,128]{3,2,1,0:T(8,128)} %bitcast.192, f32[180,32,128]{2,1,0:T(8,128)S(1)} %bitcast.195, f32[180,32,128]{2,1,0:T(8,128)S(1)} %bitcast.196, f32[180,32,128]{2,1,0:T(8,128)S(1)} %bitcast.197, f32[5,180,8,128]{3,2,1,0:T(8,128)S(1)} %copy-done.2, ...), custom_call_target="tpu_custom_call" | custom-call | flops 110592000 | bytes 41287680 | tf_op jit(solution)/shard_map/stencil/pallas_call | solution.py:369
  (116 shorter events, 23.2 us)
Async XLA Ops:
  2.7 31.1 %collective-permute-start.1 = (f32[6,2,1024]{2,1,0:T(2,128)}, f32[6,2,1024]{2,1,0:T(2,128)}, u32[]{:S(2)}, u32[]{:S(2)}) collective-permute-start(f32[6,2,1024]{2,1,0:T(2,128)} %maximum_select_fusion.1), channel_id=1, source_target_pairs={{0,1},{1,0},{2,3},{3,2},{4,5},{5,4},{6,7},{7,6},{8,9},{9,8},{10,11... | collective-permute-start | bytes 147464 | tf_op jit(solution)/shard_map/ppermute | solution.py:408
  11.9 4.2 %copy-start.9 = (f32[5,4,180,32]{2,3,1,0:T(8,128)}, f32[5,4,180,32]{2,3,1,0:T(8,128)S(1)}, u32[]{:S(2)}) copy-start(f32[5,4,180,32]{2,3,1,0:T(8,128)S(1)} %copy.70) | copy-start | bytes 1382404
  14.5 1.6 copy-start.11
  15.9 19.5 %collective-permute-start = (f32[6,64,180]{2,1,0:T(8,128)}, f32[6,64,180]{2,1,0:T(8,128)}, u32[]{:S(2)}, u32[]{:S(2)}) collective-permute-start(f32[6,64,180]{2,1,0:T(8,128)} %maximum_select_fusion), channel_id=1, source_target_pairs={{0,1},{1,0},{2,3},{3,2},{4,5},{5,4},{6,7},{7,6},{8,9},{9,8},{10,11... | collective-permute-start | bytes 829448 | tf_op jit(solution)/shard_map/ppermute | solution.py:408
  18.0 3.1 %copy-start.19 = (s32[64]{0:T(128)S(1)}, s32[64]{0:T(128)}, u32[]{:S(2)}) copy-start(s32[64]{0:T(128)} %param.15) | copy-start | bytes 772
  18.0 3.2 %copy-start.18 = (f32[384]{0:T(512)S(1)}, f32[384]{0:T(512)}, u32[]{:S(2)}) copy-start(f32[384]{0:T(512)} %constant.57) | copy-start | bytes 4612
  18.0 5.6 %copy-start.1 = (f32[4,180,1024]{2,0,1:T(4,128)S(1)}, f32[4,180,1024]{2,0,1:T(4,128)}, u32[]{:S(2)}) copy-start(f32[4,180,1024]{2,0,1:T(4,128)} %param.14) | copy-start | bytes 8847364
  23.6 5.2 %copy-start = (f32[5,4,180,1024]{3,1,2,0:T(4,128)S(1)}, f32[5,4,180,1024]{3,1,2,0:T(4,128)}, u32[]{:S(2)}) copy-start(f32[5,4,180,1024]{3,1,2,0:T(4,128)} %param.11) | copy-start | bytes 44236804
  28.8 10.3 %copy-start.14 = (f32[5,3,64,180]{3,2,1,0:T(8,128)S(1)}, f32[5,3,64,180]{3,2,1,0:T(8,128)}, u32[]{:S(2)}) copy-start(f32[5,3,64,180]{3,2,1,0:T(8,128)} %get-tuple-element.34) | copy-start | bytes 2073604
  28.8 10.3 %copy-start.15 = (f32[5,3,64,180]{3,2,1,0:T(8,128)S(1)}, f32[5,3,64,180]{3,2,1,0:T(8,128)}, u32[]{:S(2)}) copy-start(f32[5,3,64,180]{3,2,1,0:T(8,128)} %get-tuple-element.35) | copy-start | bytes 2073604
  33.7 5.4 %copy-start.10 = (f32[5,4,180,32]{2,3,1,0:T(8,128)S(1)}, f32[5,4,180,32]{2,3,1,0:T(8,128)}, u32[]{:S(2)}) copy-start(f32[5,4,180,32]{2,3,1,0:T(8,128)} %copy-done.9) | copy-start | bytes 1382404
  33.8 5.4 %copy-start.12 = (f32[5,4,180,32]{2,3,1,0:T(8,128)S(1)}, f32[5,4,180,32]{2,3,1,0:T(8,128)}, u32[]{:S(2)}) copy-start(f32[5,4,180,32]{2,3,1,0:T(8,128)} %copy-done.11) | copy-start | bytes 1382404
  39.5 1.4 copy-start.17
  39.5 97.3 %collective-permute-start.4 = (f32[6,180,8,128]{3,2,1,0:T(8,128)}, f32[6,180,8,128]{3,2,1,0:T(8,128)}, u32[]{:S(2)}, u32[]{:S(2)}) collective-permute-start(f32[6,180,8,128]{3,2,1,0:T(8,128)} %edges.1), channel_id=1, source_target_pairs={{0,1},{1,0},{2,3},{3,2},{4,5},{5,4},{6,7},{7,6},{8,9},{9,8},{10,11... | collective-permute-start | bytes 13271048 | tf_op jit(solution)/shard_map/ppermute | solution.py:459
  41.1 1.3 copy-start.16
  50.5 2.9 %slice-start = ((f32[16,80,180]{2,1,0:T(8,128)}), f32[16,80,52]{2,1,0:T(8,128)S(1)}, s32[]{:S(2)}) async-start(f32[16,80,180]{2,1,0:T(8,128)} %reshape.238), calls=%async_computation | async-start | bytes 1310720 | tf_op jit(solution)/shard_map/slice | solution.py:140
  50.5 3.0 %slice-start.1 = ((f32[16,80,180]{2,1,0:T(8,128)}), f32[16,80,128]{2,1,0:T(8,128)S(1)}, s32[]{:S(2)}) async-start(f32[16,80,180]{2,1,0:T(8,128)} %reshape.238), calls=%async_computation.1 | async-start | bytes 1310720 | tf_op jit(solution)/shard_map/slice | solution.py:141
  51.5 84.0 %collective-permute-start.2 = (f32[24,1024]{1,0:T(8,128)S(1)}, f32[24,1024]{1,0:T(8,128)S(1)}, u32[]{:S(2)}, u32[]{:S(2)}) collective-permute-start(f32[24,1024]{1,0:T(8,128)S(1)} %get-tuple-element.46), channel_id=1, source_target_pairs={{0,2},{2,4},{4,6},{6,8},{8,10},{10,12},{12,14},{14,16},{16,18},{18... | collective-permute-start | bytes 294920 | tf_op jit(solution)/shard_map/ppermute | solution.py:476
  52.9 82.8 %collective-permute-start.3 = (f32[24,1024]{1,0:T(8,128)S(1)}, f32[24,1024]{1,0:T(8,128)S(1)}, u32[]{:S(2)}, u32[]{:S(2)}) collective-permute-start(f32[24,1024]{1,0:T(8,128)S(1)} %get-tuple-element.47), channel_id=1, source_target_pairs={{2,0},{4,2},{6,4},{8,6},{10,8},{12,10},{14,12},{16,14},{18,16},{20... | collective-permute-start | bytes 294920 | tf_op jit(solution)/shard_map/ppermute | solution.py:476
  53.4 1.3 copy-start.6
  53.4 1.3 copy-start.7
  136.8 2.0 %copy-start.2 = (f32[5,180,8,128]{3,2,1,0:T(8,128)S(1)}, f32[5,180,8,128]{3,2,1,0:T(8,128)}, u32[]{:S(2)}) copy-start(f32[5,180,8,128]{3,2,1,0:T(8,128)} %fusion.smooth) | copy-start | bytes 11059204
  138.9 1.8 %copy-start.3 = (f32[4,180,1024]{2,0,1:T(4,128)S(1)}, f32[4,180,1024]{2,0,1:T(4,128)}, u32[]{:S(2)}) copy-start(f32[4,180,1024]{2,0,1:T(4,128)} %param.12) | copy-start | bytes 8847364
  140.7 1.8 %copy-start.4 = (f32[4,180,1024]{2,0,1:T(4,128)S(1)}, f32[4,180,1024]{2,0,1:T(4,128)}, u32[]{:S(2)}) copy-start(f32[4,180,1024]{2,0,1:T(4,128)} %param.13) | copy-start | bytes 8847364
  (4 other events, 4.5 us)
